TPU v7x, 32 devices: a whole 2x2x4 slice. The times are simulated.
32 devices in a mesh: groups: 2 (over y), seq: 8 (over z, x), head: 1, sub: 2 (over core).
Axes of the slice: x: 2, y: 2, z: 4, core: 2. Of those that a mesh axis runs over, the one named last changes fastest.
Arguments:
- queries: bfloat16 [8192, 16, 128], P(('groups', 'seq'), ('head', 'sub')), parts along dimension 0, may hold values from -8 to 8
- key_rows: bfloat16 [8192, 16, 128], P(('groups', 'seq'), ('head', 'sub')), parts along dimension 0, may hold values from -8 to 8
- value_rows: bfloat16 [8192, 16, 128], P(('groups', 'seq'), ('head', 'sub')), parts along dimension 0, may hold values from -6 to 6
- grad_out: bfloat16 [8192, 16, 128], P(('groups', 'seq'), ('head', 'sub')), parts along dimension 0, may hold values from -6 to 6
- global_blocks: int32 [16], P('groups'), parts along dimension 0, may hold values from 0 to 15, as said below
Outputs:
- attended: bfloat16 [8192, 16, 128], P(('groups', 'seq'), ('head', 'sub')), parts along dimension 0
- grad_queries: bfloat16 [8192, 16, 128], P(('groups', 'seq'), ('head', 'sub')), parts along dimension 0
- grad_keys: bfloat16 [8192, 16, 128], P(('groups', 'seq'), ('head', 'sub')), parts along dimension 0
- grad_values: bfloat16 [8192, 16, 128], P(('groups', 'seq'), ('head', 'sub')), parts along dimension 0
There are 2 independent parts, one for each index of `groups`. A program takes and returns all parts, laid end to end along the dimension named above; each array names one. Nothing has to cross between parts.
Inputs may be any that keep to these rules, and one draw needn't show every extreme that they name: `global_blocks`: 8 different block indices in no fixed order; block 0 and block 15 are always among them.
All inputs are finite; a program needn't handle non-finite values.
Results may differ from a plain program's by a relative error of at most 0.025.
Values may be sent and summed in bfloat16 or wider, within the bound.
A program may use at most 256 MiB of HBM per device.

v0:
```python
import math

import jax
import jax.numpy as jnp
from jax import lax
from jax.sharding import PartitionSpec as P

BLOCK = 256


def shortened(array):

    def short(part):
        return part.astype(jnp.bfloat16) if part.dtype == jnp.float32 else part

    return jax.tree.map(short, array)


def from_partner(value, axis, bit):
    mask = 2**bit
    pairs = [(source, source ^ mask) for source in range(lax.axis_size(axis))]
    return lax.ppermute(value, axis, pairs)


def spread(array, axis, root):
    mine = lax.axis_index(axis) == root
    return lax.psum(jnp.where(mine, array, jnp.zeros_like(array)), axis)


def flip_pairs(array, bit_index):
    block_count = array.shape[0]
    stride = 1 << bit_index
    shaped = array.reshape((block_count // (2 * stride), 2, stride) + array.shape[1:])
    return jnp.flip(shaped, 1).reshape(array.shape)


def fetch_first(pair, bit_index):
    return jax.tree.map(
        lambda part, own: part.astype(own.dtype),
        from_partner(shortened(pair), "seq", bit_index),
        pair,
    )


def partner_stack(key_blocks, value_blocks, inner_bits, level_count, fetcher):
    key_list = [key_blocks]
    value_list = [value_blocks]
    for level_index in range(level_count):
        if level_index < inner_bits:
            key_list.append(flip_pairs(key_blocks, level_index))
            value_list.append(flip_pairs(value_blocks, level_index))
        else:
            far_keys, far_values = fetcher((key_blocks, value_blocks), level_index - inner_bits)
            key_list.append(far_keys)
            value_list.append(far_values)
    return (jnp.stack(key_list, 1), jnp.stack(value_list, 1))


def group_logits(query_group, key_group, global_keys, keep_group, scaling):
    near_part = jnp.einsum(
        "gqhd,glkhd->ghqlk", query_group, key_group, preferred_element_type=jnp.float32
    )
    far_part = jnp.einsum(
        "gqhd,nkhd->ghqnk", query_group, global_keys, preferred_element_type=jnp.float32
    )
    far_part = jnp.where(keep_group[:, None, None, :, None], far_part * scaling, -jnp.inf)
    lead_shape = near_part.shape[:3]
    return jnp.concatenate(
        [near_part.reshape(lead_shape + (-1,)) * scaling, far_part.reshape(lead_shape + (-1,))], -1
    )


def split_keys(array, slot_count, block_rows):
    lead_shape = array.shape[:3]
    near_part = array[..., : slot_count * block_rows].reshape(lead_shape + (slot_count, block_rows))
    far_part = array[..., slot_count * block_rows :].reshape(lead_shape + (-1, block_rows))
    return (near_part, far_part)


def on_device(queries, key_rows, value_rows, grad_out, global_blocks):
    row_count, head_count, head_width = queries.shape
    block_count = row_count // BLOCK
    seq_count = lax.axis_size("seq")
    total_blocks = block_count * seq_count
    level_count = total_blocks.bit_length() - 1
    inner_bits = block_count.bit_length() - 1
    slot_count = 1 + level_count
    global_count = global_blocks.shape[0]
    scaling = 1.0 / math.sqrt(head_width)
    first_block = lax.axis_index("seq") * block_count
    block_shape = (block_count, BLOCK, head_count, head_width)
    query_blocks = queries.reshape(block_shape)
    key_blocks = key_rows.reshape(block_shape)
    value_blocks = value_rows.reshape(block_shape)
    grad_blocks = grad_out.reshape(block_shape)
    block_ids = first_block + jnp.arange(block_count, dtype=jnp.int32)
    xor_offsets = jnp.bitwise_xor(global_blocks[None, :], block_ids[:, None])
    keep_global = jnp.bitwise_and(xor_offsets, xor_offsets - 1) != 0
    picked_keys = []
    picked_values = []
    for member in range(global_count):
        target = global_blocks[member]
        local_index = target % block_count
        key_single = lax.dynamic_index_in_dim(key_blocks, local_index, 0, keepdims=False)
        value_single = lax.dynamic_index_in_dim(value_blocks, local_index, 0, keepdims=False)
        key_got, value_got = (
            spread(key_single, "seq", target // block_count),
            spread(value_single, "seq", target // block_count),
        )
        picked_keys.append(key_got)
        picked_values.append(value_got)
    global_keys = jnp.stack(picked_keys, 0)
    global_values = jnp.stack(picked_values, 0)
    key_stack, value_stack = partner_stack(
        key_blocks, value_blocks, inner_bits, level_count, fetch_first
    )
    pair_count = block_count // 2

    def grouped(array):
        return array.reshape((pair_count, 2) + array.shape[1:])

    def forward_group(operands):
        query_group, key_group, value_group, keep_group = operands
        logits = group_logits(query_group, key_group, global_keys, keep_group, scaling)
        row_peak = jnp.max(logits, -1, keepdims=True)
        log_total = row_peak + jnp.log(jnp.sum(jnp.exp(logits - row_peak), -1, keepdims=True))
        weights = jnp.exp(logits - log_total).astype(jnp.bfloat16)
        near_weights, far_weights = split_keys(weights, slot_count, BLOCK)
        output = jnp.einsum(
            "ghqlk,glkhd->gqhd", near_weights, value_group, preferred_element_type=jnp.float32
        )
        output = output + jnp.einsum(
            "ghqnk,nkhd->gqhd", far_weights, global_values, preferred_element_type=jnp.float32
        )
        return (output.astype(jnp.bfloat16), log_total)

    attended_groups, log_totals = lax.map(
        forward_group,
        (grouped(query_blocks), grouped(key_stack), grouped(value_stack), grouped(keep_global)),
    )

    def backward_group(carried, operands):
        key_sum_now, value_sum_now = carried
        query_group, key_group, value_group, keep_group, grad_group, output_group, total_group = (
            operands
        )
        logits = group_logits(query_group, key_group, global_keys, keep_group, scaling)
        weights = jnp.exp(logits - total_group)
        weights_low = weights.astype(jnp.bfloat16)
        row_delta = jnp.sum(
            grad_group.astype(jnp.float32) * output_group.astype(jnp.float32), -1
        ).transpose(0, 2, 1)
        near_grad = jnp.einsum(
            "gqhd,glkhd->ghqlk", grad_group, value_group, preferred_element_type=jnp.float32
        )
        far_grad = jnp.einsum(
            "gqhd,nkhd->ghqnk", grad_group, global_values, preferred_element_type=jnp.float32
        )
        lead_shape = near_grad.shape[:3]
        grad_weights = jnp.concatenate(
            [near_grad.reshape(lead_shape + (-1,)), far_grad.reshape(lead_shape + (-1,))], -1
        )
        grad_logits = (weights * (grad_weights - row_delta[..., None]) * scaling).astype(
            jnp.bfloat16
        )
        near_logit, far_logit = split_keys(grad_logits, slot_count, BLOCK)
        near_weight, far_weight = split_keys(weights_low, slot_count, BLOCK)
        grad_query = jnp.einsum(
            "ghqlk,glkhd->gqhd", near_logit, key_group, preferred_element_type=jnp.float32
        )
        grad_query = grad_query + jnp.einsum(
            "ghqnk,nkhd->gqhd", far_logit, global_keys, preferred_element_type=jnp.float32
        )
        key_terms = jnp.einsum(
            "ghqlk,gqhd->glkhd", near_logit, query_group, preferred_element_type=jnp.float32
        )
        value_terms = jnp.einsum(
            "ghqlk,gqhd->glkhd", near_weight, grad_group, preferred_element_type=jnp.float32
        )
        key_sum_now = key_sum_now + jnp.einsum(
            "ghqnk,gqhd->nkhd", far_logit, query_group, preferred_element_type=jnp.float32
        )
        value_sum_now = value_sum_now + jnp.einsum(
            "ghqnk,gqhd->nkhd", far_weight, grad_group, preferred_element_type=jnp.float32
        )
        return (
            (key_sum_now, value_sum_now),
            (grad_query.astype(jnp.bfloat16), key_terms, value_terms),
        )

    global_zeros = jnp.zeros((global_count, BLOCK, head_count, head_width), jnp.float32)
    global_terms, back_outputs = lax.scan(
        backward_group,
        (global_zeros, global_zeros),
        (
            grouped(query_blocks),
            grouped(key_stack),
            grouped(value_stack),
            grouped(keep_global),
            grouped(grad_blocks),
            attended_groups,
            log_totals,
        ),
    )
    grad_query_groups, key_term_groups, value_term_groups = back_outputs
    slot_shape = (block_count, slot_count, BLOCK, head_count, head_width)
    key_terms_all = key_term_groups.reshape(slot_shape)
    value_terms_all = value_term_groups.reshape(slot_shape)
    grad_key_sum = key_terms_all[:, 0]
    grad_value_sum = value_terms_all[:, 0]
    for level_index in range(level_count):
        key_term = key_terms_all[:, 1 + level_index]
        value_term = value_terms_all[:, 1 + level_index]
        if level_index < inner_bits:
            grad_key_sum = grad_key_sum + flip_pairs(key_term, level_index)
            grad_value_sum = grad_value_sum + flip_pairs(value_term, level_index)
        else:
            back_key, back_value = from_partner(
                (key_term.astype(jnp.bfloat16), value_term.astype(jnp.bfloat16)),
                "seq",
                level_index - inner_bits,
            )
            grad_key_sum = grad_key_sum + back_key.astype(jnp.float32)
            grad_value_sum = grad_value_sum + back_value.astype(jnp.float32)
    key_partial = global_terms[0].astype(jnp.bfloat16).astype(jnp.float32)
    value_partial = global_terms[1].astype(jnp.bfloat16).astype(jnp.float32)
    key_share, value_share = (
        lax.psum_scatter(
            key_partial.astype(jnp.bfloat16), "seq", scatter_dimension=1, tiled=True
        ).astype(jnp.float32),
        lax.psum_scatter(
            value_partial.astype(jnp.bfloat16), "seq", scatter_dimension=1, tiled=True
        ).astype(jnp.float32),
    )
    every_block = jnp.arange(total_blocks, dtype=jnp.int32)
    route_weight = (
        (global_blocks[:, None] == every_block[None, :])
        .astype(jnp.float32)
        .T[:, :, None, None, None]
    )
    key_send = jnp.sum(route_weight * key_share[None], 1)
    value_send = jnp.sum(route_weight * value_share[None], 1)
    key_owned, value_owned = (
        lax.all_to_all(
            key_send.astype(jnp.bfloat16), "seq", split_axis=0, concat_axis=1, tiled=True
        ).astype(key_send.dtype),
        lax.all_to_all(
            value_send.astype(jnp.bfloat16), "seq", split_axis=0, concat_axis=1, tiled=True
        ).astype(value_send.dtype),
    )
    grad_key_sum = grad_key_sum + key_owned
    grad_value_sum = grad_value_sum + value_owned
    return (
        attended_groups.reshape(queries.shape),
        grad_query_groups.reshape(queries.shape),
        grad_key_sum.astype(jnp.bfloat16).reshape(queries.shape),
        grad_value_sum.astype(jnp.bfloat16).reshape(queries.shape),
    )


def solution(mesh):
    in_specs = (
        P(("groups", "seq"), ("head", "sub"), None),
        P(("groups", "seq"), ("head", "sub"), None),
        P(("groups", "seq"), ("head", "sub"), None),
        P(("groups", "seq"), ("head", "sub"), None),
        P("groups"),
    )
    out_specs = (
        P(("groups", "seq"), ("head", "sub"), None),
        P(("groups", "seq"), ("head", "sub"), None),
        P(("groups", "seq"), ("head", "sub"), None),
        P(("groups", "seq"), ("head", "sub"), None),
    )
    return jax.shard_map(
        on_device, mesh=mesh, in_specs=in_specs, out_specs=out_specs, check_vma=False
    )
```

profile of v0, /device:TPU:8, one launch (start us, length us, event | category | flops | bytes accessed | tf_op | source)
XLA Modules:
  0.0 984.0 jit_solution(14491541534180600365)
XLA Ops:
  58.8 27.3 %collective-permute-done.3 = bf16[2,256,8,128]{3,1,2,0:T(8,128)(2,1)} collective-permute-done((bf16[2,256,8,128]{3,1,2,0:T(8,128)(2,1)}, bf16[2,256,8,128]{3,1,2,0:T(8,128)(2,1)}, u32[]{:S(2)}, u32[]{:S(2)}) %collective-permute-start.3) | collective-permute-done | bytes 1048608 | tf_op jit(solution)/shard_map/ppermute | solution.py:22
  90.2 42.1 %collective-permute-done.4 = bf16[2,256,8,128]{3,1,2,0:T(8,128)(2,1)} collective-permute-done((bf16[2,256,8,128]{3,1,2,0:T(8,128)(2,1)}, bf16[2,256,8,128]{3,1,2,0:T(8,128)(2,1)}, u32[]{:S(2)}, u32[]{:S(2)}) %collective-permute-start.4) | collective-permute-done | bytes 1048608 | tf_op jit(solution)/shard_map/ppermute | solution.py:22
  141.7 79.2 %collective-permute-done.1 = bf16[2,256,8,128]{1,3,2,0:T(8,128)(2,1)} collective-permute-done((bf16[2,256,8,128]{1,3,2,0:T(8,128)(2,1)}, bf16[2,256,8,128]{1,3,2,0:T(8,128)(2,1)}, u32[]{:S(2)}, u32[]{:S(2)}) %collective-permute-start.1) | collective-permute-done | bytes 1048608 | tf_op jit(solution)/shard_map/ppermute | solution.py:22
  235.2 8.9 fusion.33
  244.1 165.1 %all-reduce.3.cloned.1.call-done = (bf16[1,256,8,128]{3,1,0,2:T(8,128)(2,1)}, bf16[1,256,8,128]{3,1,0,2:T(8,128)(2,1)}, bf16[1,256,8,128]{3,1,0,2:T(8,128)(2,1)}...) async-done(((bf16[1,256,8,128]{3,1,0,2:T(8,128)(2,1)}, ...) | async-done | bytes 8388624 | tf_op jit(solution)/shard_map/psum | solution.py:27
  415.2 13.1 %fusion.43 = (f32[2,8,256]{2,0,1:T(2,128)S(1)}, f32[2,8,256,8,256]{2,4,0,3,1:T(8,128)}) fusion(bf16[2,256,8,128,1]{3,2,1,0,4:T(8,128)(2,1)S(1)} %bitcast.232, bf16[8,256,8,128]{3,1,0,2:T(8,128)(2,1)S(1)} %constant_dynamic-update-slice_fusion.1, pred[2,8]{0,1:T(8,128)(4,1)S(1)} %fusion.40), kind=kOutput, calls=%fused_computation.134 | convolution fusion | flops 2172645376 | bytes 38813712 | tf_op jit(solution)/shard_map/while/body/eval_jaxpr/gqhd,nkhd->ghqnk/dot_general | solution.py:63
  428.3 22.8 %copy.255 = f32[2,8,256,8,256]{2,4,3,1,0:T(8,128)} copy(f32[2,8,256,8,256]{2,4,0,3,1:T(8,128)} %get-tuple-element.127) | data formatting | bytes 67108864 | tf_op jit(solution)/shard_map/while/body/eval_jaxpr/jit(_where)/select_n | solution.py:66
  451.1 17.3 %exponential_reduce_fusion = f32[2,8,256]{2,1,0:T(8,128)S(1)} fusion(f32[2,8,256,2048]{2,3,1,0:T(8,128)} %bitcast.235, f32[2,8,256,1280]{2,3,1,0:T(8,128)} %bitcast.238, f32[2,8,256]{2,1,0:T(8,128)S(1)} %copy_maximum_fusion), kind=kLoop, calls=%fused_computation.6 | loop fusion | flops 40890368 | bytes 54558720 | tf_op jit(solution)/shard_map/while/body/eval_jaxpr/reduce_sum | solution.py:126
  468.4 27.0 %fusion.3 = bf16[2,8,256,3328]{2,3,1,0:T(8,128)(2,1)} fusion(f32[2,8,256,2048]{2,3,1,0:T(8,128)} %bitcast.236, f32[2,8,256,1280]{2,3,1,0:T(8,128)} %bitcast.239, f32[2,8,256]{2,1,0:T(8,128)S(1)} %log_add_fusion), kind=kLoop, calls=%fused_computation.7 | loop fusion | flops 40894464 | bytes 81805312 | tf_op jit(solution)/shard_map/while/body/eval_jaxpr/convert_element_type | solution.py:127
  495.4 14.0 %slice.103 = bf16[2,8,256,2048]{2,3,1,0:T(8,128)(2,1)} slice(bf16[2,8,256,3328]{2,3,1,0:T(8,128)(2,1)} %fusion.3), slice={[0:2], [0:8], [0:256], [1280:3328]} | slice | bytes 33554432 | tf_op jit(solution)/shard_map/while/body/eval_jaxpr/slice | solution.py:76
  509.5 8.9 slice.102
  528.9 17.9 %convolution_bitcast_fusion = f32[2,8,256,8,256]{2,4,0,3,1:T(8,128)} fusion(bf16[8,256,8,128]{3,1,0,2:T(8,128)(2,1)} %constant_dynamic-update-slice_fusion.9, bf16[2,256,8,128,1]{3,2,1,0,4:T(8,128)(2,1)S(1)} %bitcast.262), kind=kOutput, calls=%fused_computation.11 | convolution fusion | flops 2147483648 | bytes 38797312 | tf_op jit(solution)/shard_map/while/body/eval_jaxpr/gqhd,nkhd->ghqnk/dot_general | solution.py:156
  546.9 9.8 fusion.8
  564.3 22.8 %copy.272 = f32[2,8,256,8,256]{2,4,3,1,0:T(8,128)} copy(f32[2,8,256,8,256]{2,4,0,3,1:T(8,128)} %convolution_bitcast_fusion) | data formatting | bytes 67108864 | tf_op jit(solution)/shard_map/while/body/eval_jaxpr/gqhd,nkhd->ghqnk/transpose | solution.py:156
  587.1 43.6 %fusion.2 = bf16[2,8,256,3328]{2,3,1,0:T(8,128)(2,1)} fusion(f32[2,8,256,2048]{2,3,1,0:T(8,128)} %bitcast.243, f32[2,8,256,1280]{2,3,1,0:T(8,128)} %bitcast.248, f32[2,8,256,2048]{2,3,1,0:T(8,128)} %bitcast.237, f32[2,8,256,1280]{2,3,1,0:T(8,128)} %bitcast.240, f32[2,8,256]{2,1,0:T(8,128)S(1)} %bitcast.272, f32[2,8,256]{2,1,0:T(8,128)S(1)} %log_add_fusion), kind=kLoop, calls=%fused_computation.4 | loop fusion | flops 95420416 | bytes 136347648 | tf_op jit(solution)/shard_map/while/body/eval_jaxpr/convert_element_type | solution.py:163
  630.7 13.8 %slice.105 = bf16[2,8,256,2048]{2,3,1,0:T(8,128)(2,1)} slice(bf16[2,8,256,3328]{2,3,1,0:T(8,128)(2,1)} %fusion.2), slice={[0:2], [0:8], [0:256], [1280:3328]} | slice | bytes 33554432 | tf_op jit(solution)/shard_map/while/body/eval_jaxpr/slice | solution.py:76
  644.5 12.2 %fusion.35 = bf16[8,8,256,128,1]{3,2,1,0,4:T(8,128)(2,1)} fusion(bf16[2,8,256,8,256]{2,4,3,1,0:T(8,128)(2,1)} %bitcast.249, bf16[2,256,8,128,1]{3,2,1,0,4:T(8,128)(2,1)S(1)} %bitcast.233), kind=kOutput, calls=%fused_computation.72 | convolution fusion | flops 2147483648 | bytes 22020096 | tf_op jit(solution)/shard_map/while/body/eval_jaxpr/ghqnk,gqhd->nkhd/dot_general | solution.py:180
  661.4 12.4 %fusion.30 = bf16[8,8,256,128,1]{3,2,1,0,4:T(8,128)(2,1)} fusion(bf16[2,8,256,8,256]{2,4,3,1,0:T(8,128)(2,1)} %bitcast.252, bf16[2,256,8,128,1]{3,2,1,0,4:T(8,128)(2,1)S(1)} %bitcast.263), kind=kOutput, calls=%fused_computation.67 | convolution fusion | flops 2147483648 | bytes 22020096 | tf_op jit(solution)/shard_map/while/body/eval_jaxpr/ghqnk,gqhd->nkhd/dot_general | solution.py:183
  678.4 9.0 slice.104
  687.4 12.9 %fusion.45 = (bf16[2,5,256,8,128]{4,2,1,3,0:T(8,128)(2,1)}, f32[2,5,256,8,128]{4,2,1,3,0:T(8,128)}) fusion(bf16[2,8,256,5,256]{2,4,3,1,0:T(8,128)(2,1)} %bitcast.244, bf16[2,256,8,128,1]{3,2,1,0,4:T(8,128)(2,1)S(1)} %bitcast.264), kind=kOutput, calls=%fused_computation.136 | convolution fusion | flops 1344798720 | bytes 27262976 | tf_op jit(solution)/shard_map/while/body/eval_jaxpr/ghqlk,gqhd->glkhd/dot_general | solution.py:177
  717.0 54.3 %reduce-scatter.3.cloned.1.call-done = bf16[8,32,8,128]{3,1,2,0:T(8,128)(2,1)} async-done(((bf16[8,256,8,128]{3,1,2,0:T(8,128)(2,1)}), bf16[8,32,8,128]{3,1,2,0:T(8,128)(2,1)}) %reduce-scatter.3.cloned.1.call-update) | async-done | bytes 524304 | tf_op jit(solution)/shard_map/reduce_scatter | solution.py:228
  772.5 92.4 %reduce-scatter.5.cloned.1.call-done = bf16[8,32,8,128]{3,1,2,0:T(8,128)(2,1)} async-done(((bf16[8,256,8,128]{3,1,2,0:T(8,128)(2,1)}), bf16[8,32,8,128]{3,1,2,0:T(8,128)(2,1)}) %reduce-scatter.5.cloned.1.call-update) | async-done | bytes 524304 | tf_op jit(solution)/shard_map/reduce_scatter | solution.py:231
  889.0 9.4 all-to-all-done.1
  937.3 35.1 %collective-permute-done.8 = bf16[2,256,8,128]{3,1,2,0:T(8,128)(2,1)} collective-permute-done((bf16[2,256,8,128]{3,1,2,0:T(8,128)(2,1)}, bf16[2,256,8,128]{3,1,2,0:T(8,128)(2,1)}, u32[]{:S(2)}, u32[]{:S(2)}) %collective-permute-start.8) | collective-permute-done | bytes 1048608 | tf_op jit(solution)/shard_map/ppermute | solution.py:22
  (153 shorter events, 178.2 us)
Async XLA Ops:
  7.2 219.4 %copy-start = (bf16[512,8,128]{2,1,0:T(8,128)(2,1)S(1)}, bf16[512,8,128]{2,1,0:T(8,128)(2,1)}, u32[]{:S(2)}) copy-start(bf16[512,8,128]{2,1,0:T(8,128)(2,1)} %param.5) | copy-start | bytes 3145732
  7.2 24.9 %copy-start.4 = (bf16[512,8,128]{2,1,0:T(8,128)(2,1)S(1)}, bf16[512,8,128]{2,1,0:T(8,128)(2,1)}, u32[]{:S(2)}) copy-start(bf16[512,8,128]{2,1,0:T(8,128)(2,1)} %param.6) | copy-start | bytes 3145732
  7.2 402.0 %all-reduce.3.cloned.1.call-start = ((), (), s32[]{:S(2)}) async-start(), calls=%async_computation.6 | async-start | bytes 16777216 | tf_op jit(solution)/shard_map/psum | solution.py:27
  41.7 729.6 %reduce-scatter.3.cloned.1.call-start = ((), (), s32[]{:S(2)}) async-start(), calls=%async_computation.4 | async-start | bytes 4718592 | tf_op jit(solution)/shard_map/reduce_scatter | solution.py:228
  43.4 42.8 %collective-permute-start.3 = (bf16[2,256,8,128]{3,1,2,0:T(8,128)(2,1)}, bf16[2,256,8,128]{3,1,2,0:T(8,128)(2,1)}, u32[]{:S(2)}, u32[]{:S(2)}) collective-permute-start(bf16[2,256,8,128]{3,1,2,0:T(8,128)(2,1)} %copy.241), channel_id=1, source_target_pairs={{0,2},{2,0},{4,6},{6,4},{8,10},{10,8},{12,14},{14,12},{1,3},{3,1},... | collective-permute-start | bytes 3145736 | tf_op jit(solution)/shard_map/ppermute | solution.py:22
  44.9 87.3 %collective-permute-start.4 = (bf16[2,256,8,128]{3,1,2,0:T(8,128)(2,1)}, bf16[2,256,8,128]{3,1,2,0:T(8,128)(2,1)}, u32[]{:S(2)}, u32[]{:S(2)}) collective-permute-start(bf16[2,256,8,128]{3,1,2,0:T(8,128)(2,1)} %copy.241), channel_id=1, source_target_pairs={{0,4},{2,6},{4,0},{6,2},{8,12},{10,14},{12,8},{14,10},{1,5},{3,7},... | collective-permute-start | bytes 3145736 | tf_op jit(solution)/shard_map/ppermute | solution.py:22
  45.3 92.8 %collective-permute-start.5 = (bf16[2,256,8,128]{3,1,2,0:T(8,128)(2,1)}, bf16[2,256,8,128]{3,1,2,0:T(8,128)(2,1)}, u32[]{:S(2)}, u32[]{:S(2)}) collective-permute-start(bf16[2,256,8,128]{3,1,2,0:T(8,128)(2,1)} %copy.241), channel_id=1, source_target_pairs={{0,8},{2,10},{4,12},{6,14},{8,0},{10,2},{12,4},{14,6},{1,9},{3,11}... | collective-permute-start | bytes 3145736 | tf_op jit(solution)/shard_map/ppermute | solution.py:22
  49.4 90.1 %collective-permute-start = (bf16[2,256,8,128]{1,3,2,0:T(8,128)(2,1)}, bf16[2,256,8,128]{1,3,2,0:T(8,128)(2,1)}, u32[]{:S(2)}, u32[]{:S(2)}) collective-permute-start(bf16[2,256,8,128]{1,3,2,0:T(8,128)(2,1)} %copy.236), channel_id=1, source_target_pairs={{0,2},{2,0},{4,6},{6,4},{8,10},{10,8},{12,14},{14,12},{1,3},{3,1},... | collective-permute-start | bytes 3145736 | tf_op jit(solution)/shard_map/ppermute | solution.py:22
  50.0 171.0 %collective-permute-start.1 = (bf16[2,256,8,128]{1,3,2,0:T(8,128)(2,1)}, bf16[2,256,8,128]{1,3,2,0:T(8,128)(2,1)}, u32[]{:S(2)}, u32[]{:S(2)}) collective-permute-start(bf16[2,256,8,128]{1,3,2,0:T(8,128)(2,1)} %copy.236), channel_id=1, source_target_pairs={{0,4},{2,6},{4,0},{6,2},{8,12},{10,14},{12,8},{14,10},{1,5},{3,7},... | collective-permute-start | bytes 3145736 | tf_op jit(solution)/shard_map/ppermute | solution.py:22
  55.6 30.6 %copy-start.11 = (bf16[2,256,8,128]{1,3,2,0:T(8,128)(2,1)S(1)}, bf16[2,256,8,128]{1,3,2,0:T(8,128)(2,1)}, u32[]{:S(2)}) copy-start(bf16[2,256,8,128]{1,3,2,0:T(8,128)(2,1)} %copy.236) | copy-start | bytes 3145732
  86.2 140.3 %collective-permute-start.2 = (bf16[2,256,8,128]{1,3,2,0:T(8,128)(2,1)S(1)}, bf16[2,256,8,128]{1,3,2,0:T(8,128)(2,1)S(1)}, u32[]{:S(2)}, u32[]{:S(2)}) collective-permute-start(bf16[2,256,8,128]{1,3,2,0:T(8,128)(2,1)S(1)} %copy-done.11), channel_id=1, source_target_pairs={{0,8},{2,10},{4,12},{6,14},{8,0},{10,2},{12,4},{14,6},{1,9},{3,11}... | collective-permute-start | bytes 3145736 | tf_op jit(solution)/shard_map/ppermute | solution.py:22
  139.5 95.6 %copy-start.2 = (bf16[2,5,256,8,128]{4,2,1,3,0:T(8,128)(2,1)}, bf16[2,5,256,8,128]{4,2,1,3,0:T(8,128)(2,1)S(1)}, u32[]{:S(2)}) copy-start(bf16[2,5,256,8,128]{4,2,1,3,0:T(8,128)(2,1)S(1)} %bitcast_dynamic-update-slice_fusion) | copy-start | bytes 15728644
  528.9 27.8 %slice-start = ((s8[10485760]{0:T(1024)(128)(4,1)}), s8[2097152]{0:T(1024)(128)(4,1)S(1)}, s32[]{:S(2)}) async-start(s8[10485760]{0:T(1024)(128)(4,1)} %bitcast.245), calls=%async_computation.7 | async-start | bytes 4194304
  528.9 27.8 %slice-start.1 = ((s8[10485760]{0:T(1024)(128)(4,1)}), s8[4194304]{0:T(1024)(128)(4,1)S(1)}, s32[]{:S(2)}) async-start(s8[10485760]{0:T(1024)(128)(4,1)} %bitcast.245), calls=%async_computation.8 | async-start | bytes 8388608
  661.3 203.5 %reduce-scatter.5.cloned.1.call-start = ((), (), s32[]{:S(2)}) async-start(), calls=%async_computation.5 | async-start | bytes 4718592 | tf_op jit(solution)/shard_map/reduce_scatter | solution.py:231
  687.4 22.1 %copy-start.1 = (bf16[2,8,256,1280]{2,3,1,0:T(8,128)(2,1)S(1)}, bf16[2,8,256,1280]{2,3,1,0:T(8,128)(2,1)}, u32[]{:S(2)}) copy-start(bf16[2,8,256,1280]{2,3,1,0:T(8,128)(2,1)} %slice.104) | copy-start | bytes 31457284
  704.0 213.0 %collective-permute-start.10 = (bf16[2,256,8,128]{3,1,2,0:T(8,128)(2,1)}, bf16[2,256,8,128]{3,1,2,0:T(8,128)(2,1)}, u32[]{:S(2)}, u32[]{:S(2)}) collective-permute-start(bf16[2,256,8,128]{3,1,2,0:T(8,128)(2,1)} %get-tuple-element.96), channel_id=1, source_target_pairs={{0,4},{2,6},{4,0},{6,2},{8,12},{10,14},{12,8},{14,10},{1,5},{3,7},... | collective-permute-start | bytes 3145736 | tf_op jit(solution)/shard_map/ppermute | solution.py:22
  706.8 218.7 %collective-permute-start.11 = (bf16[2,256,8,128]{3,1,2,0:T(8,128)(2,1)}, bf16[2,256,8,128]{3,1,2,0:T(8,128)(2,1)}, u32[]{:S(2)}, u32[]{:S(2)}) collective-permute-start(bf16[2,256,8,128]{3,1,2,0:T(8,128)(2,1)} %get-tuple-element.80), channel_id=1, source_target_pairs={{0,8},{2,10},{4,12},{6,14},{8,0},{10,2},{12,4},{14,6},{1,9},{3,11}... | collective-permute-start | bytes 3145736 | tf_op jit(solution)/shard_map/ppermute | solution.py:22
  707.7 217.8 %collective-permute-start.9 = (bf16[2,256,8,128]{3,1,2,0:T(8,128)(2,1)}, bf16[2,256,8,128]{3,1,2,0:T(8,128)(2,1)}, u32[]{:S(2)}, u32[]{:S(2)}) collective-permute-start(bf16[2,256,8,128]{3,1,2,0:T(8,128)(2,1)} %get-tuple-element.79), channel_id=1, source_target_pairs={{0,2},{2,0},{4,6},{6,4},{8,10},{10,8},{12,14},{14,12},{1,3},{3,1},... | collective-permute-start | bytes 3145736 | tf_op jit(solution)/shard_map/ppermute | solution.py:22
  870.1 28.4 %all-to-all-start.1 = ((bf16[16,32,8,128]{3,2,1,0:T(8,128)(2,1)}), bf16[16,32,8,128]{3,2,1,0:T(8,128)(2,1)}, u32[]{:S(2)}, u32[]{:S(2)}) async-start(bf16[16,32,8,128]{3,2,1,0:T(8,128)(2,1)} %get-tuple-element.46), calls=%async_computation.3 | async-start | bytes 2097152 | tf_op jit(solution)/shard_map/all_to_all | solution.py:247
  878.5 58.8 %collective-permute-start.6 = (bf16[2,256,8,128]{3,1,2,0:T(8,128)(2,1)}, bf16[2,256,8,128]{3,1,2,0:T(8,128)(2,1)}, u32[]{:S(2)}, u32[]{:S(2)}) collective-permute-start(bf16[2,256,8,128]{3,1,2,0:T(8,128)(2,1)} %get-tuple-element.97), channel_id=1, source_target_pairs={{0,2},{2,0},{4,6},{6,4},{8,10},{10,8},{12,14},{14,12},{1,3},{3,1},... | collective-permute-start | bytes 3145736 | tf_op jit(solution)/shard_map/ppermute | solution.py:22
  880.0 57.4 %collective-permute-start.7 = (bf16[2,256,8,128]{3,1,2,0:T(8,128)(2,1)}, bf16[2,256,8,128]{3,1,2,0:T(8,128)(2,1)}, u32[]{:S(2)}, u32[]{:S(2)}) collective-permute-start(bf16[2,256,8,128]{3,1,2,0:T(8,128)(2,1)} %get-tuple-element.99), channel_id=1, source_target_pairs={{0,4},{2,6},{4,0},{6,2},{8,12},{10,14},{12,8},{14,10},{1,5},{3,7},... | collective-permute-start | bytes 3145736 | tf_op jit(solution)/shard_map/ppermute | solution.py:22
  898.4 37.0 %all-to-all-start = ((bf16[16,32,8,128]{3,2,1,0:T(8,128)(2,1)}), bf16[16,32,8,128]{3,2,1,0:T(8,128)(2,1)}, u32[]{:S(2)}, u32[]{:S(2)}) async-start(bf16[16,32,8,128]{3,2,1,0:T(8,128)(2,1)} %get-tuple-element.47), calls=%async_computation.1 | async-start | bytes 2097152 | tf_op jit(solution)/shard_map/all_to_all | solution.py:244
  916.9 55.5 %collective-permute-start.8 = (bf16[2,256,8,128]{3,1,2,0:T(8,128)(2,1)}, bf16[2,256,8,128]{3,1,2,0:T(8,128)(2,1)}, u32[]{:S(2)}, u32[]{:S(2)}) collective-permute-start(bf16[2,256,8,128]{3,1,2,0:T(8,128)(2,1)} %get-tuple-element.98), channel_id=1, source_target_pairs={{0,8},{2,10},{4,12},{6,14},{8,0},{10,2},{12,4},{14,6},{1,9},{3,11}... | collective-permute-start | bytes 3145736 | tf_op jit(solution)/shard_map/ppermute | solution.py:22
  (18 other events, 141.1 us)
Sparse Core Ops, SparseCore 0:
  41.8 367.4 all-reduce.2
  661.5 109.7 reduce-scatter.2
  774.9 89.9 reduce-scatter.4
where the time goes:
time: 993 us; the launch traced here: 984 us
  waiting for transfers between devices  519 us (52%)
  local copies, waits for them, and re-layouts  162 us (16%)
  matrix products  125 us (13%)
  other arithmetic  113 us (11%)
  between operations  34.5 us (3%)
  starting transfers between devices  31.3 us (3%)
    ppermute x12, waiting for transfers between devices, from_partner(): return lax.ppermute(value, axis, pairs)  192 us
    psum x1, waiting for transfers between devices, spread(): return lax.psum(jnp.where(mine, array, jnp.zeros_like(array)), axis)  165 us
    reduce_scatter x1, waiting for transfers between devices, on_device(): lax.psum_scatter(value_partial.astype(jnp.bfloat16), 'seq', scatter_dimen...  92.4 us
    reduce_scatter x1, waiting for transfers between devices, on_device(): lax.psum_scatter(key_partial.astype(jnp.bfloat16), 'seq', scatter_dimensi...  54.3 us
    convert_element_type x1, other arithmetic, backward_group(): (weights * (grad_weights - row_delta[..., None]) * scaling).astype(jnp.bf...  43.6 us
    unnamed x74, local copies, waits for them, and re-layouts  29.8 us
    slice x2, local copies, waits for them, and re-layouts, split_keys(): array[..., slot_count * block_rows:].reshape(lead_shape + (-1, block_rows))  27.8 us
    convert_element_type x1, other arithmetic, forward_group(): weights = jnp.exp(logits - log_total).astype(jnp.bfloat16)  27 us
  transfers between devices with their start and end apart: 17, of which 11 were waited for; matrix products, arithmetic and copies ran while one was open for 13% of the time, Pallas kernels for 0%

commit v1 on v0

--- a/solution.py
+++ b/solution.py
@@ -1,8 +1,11 @@
+import functools
 import math
 
 import jax
 import jax.numpy as jnp
 from jax import lax
+from jax.experimental import pallas as pl
+from jax.experimental.pallas import tpu as pltpu
 from jax.sharding import PartitionSpec as P
 
 BLOCK = 256
@@ -77,7 +80,7 @@
     return (near_part, far_part)
 
 
-def on_device(queries, key_rows, value_rows, grad_out, global_blocks):
+def gathered_plan(queries, key_rows, value_rows, grad_out, global_blocks):
     row_count, head_count, head_width = queries.shape
     block_count = row_count // BLOCK
     seq_count = lax.axis_size("seq")
@@ -258,6 +261,197 @@
     )
 
 
+NT = (((1,), (1,)), ((), ()))
+NN = (((1,), (0,)), ((), ()))
+
+
+def product(left, right, dims):
+    return lax.dot_general(left, right, dims, preferred_element_type=jnp.float32)
+
+
+def head_kernel(
+    level_count,
+    inner_bits,
+    scaling,
+    globals_ref,
+    query_ref,
+    grad_ref,
+    key_ref,
+    value_ref,
+    out_ref,
+    key_flip,
+    value_flip,
+    key_sum,
+    value_sum,
+    logit_ref,
+    weight_ref,
+    table_ref,
+):
+    block = pl.program_id(0)
+    total_blocks = key_flip.shape[0]
+    width = key_flip.shape[1]
+    inner_mask = (1 << inner_bits) - 1
+    near_count = 1 + level_count
+    global_count = globals_ref.shape[0]
+    factor = scaling * math.log2(math.e)
+
+    @pl.when(block == 0)
+    def _():
+        def prepare(index, carry):
+            major, minor = index >> inner_bits, index & inner_mask
+            key_flip[index] = key_ref[major, 0, minor].astype(jnp.float32).T.astype(jnp.bfloat16)
+            value_flip[index] = (
+                value_ref[major, 0, minor].astype(jnp.float32).T.astype(jnp.bfloat16)
+            )
+            key_sum[index] = jnp.zeros((BLOCK, width), jnp.float32)
+            value_sum[index] = jnp.zeros((BLOCK, width), jnp.float32)
+            return carry
+
+        lax.fori_loop(0, total_blocks, prepare, 0)
+
+    kept = jnp.int32(0)
+    for member in range(global_count):
+        target = globals_ref[member]
+        offset = target ^ block
+        table_ref[kept] = target
+        kept = kept + ((offset & (offset - 1)) != 0).astype(jnp.int32)
+    slot_total = near_count + kept
+    fixed_count = near_count + max(0, global_count - near_count)
+
+    def block_of(slot):
+        if isinstance(slot, int) and slot < near_count:
+            return block ^ (0 if slot == 0 else 1 << (slot - 1))
+        return table_ref[slot - near_count]
+
+    def over_slots(body, carry):
+        for slot in range(fixed_count):
+            carry = body(slot, carry)
+        return lax.fori_loop(fixed_count, slot_total, body, carry)
+
+    query = query_ref[0, 0, 0]
+    grad = grad_ref[0, 0, 0]
+
+    def logits_step(slot, peak):
+        index = block_of(slot)
+        keys = key_ref[index >> inner_bits, 0, index & inner_mask]
+        logits = product(keys, query, NT)
+        logit_ref[slot] = logits
+        return jnp.maximum(peak, jnp.max(logits.reshape(BLOCK // 8, 8, BLOCK), 0))
+
+    peak = over_slots(logits_step, jnp.full((8, BLOCK), -jnp.inf, jnp.float32))
+    peak = jnp.max(peak, 0, keepdims=True) * factor
+
+    def weights_step(slot, carry):
+        total, output = carry
+        weights = jnp.exp2(logit_ref[slot] * factor - peak)
+        total = total + jnp.sum(weights.reshape(BLOCK // 8, 8, BLOCK), 0)
+        weights = weights.astype(jnp.bfloat16)
+        weight_ref[slot] = weights
+        return (total, output + product(value_flip[block_of(slot)], weights, NN))
+
+    total, output = over_slots(
+        weights_step,
+        (jnp.zeros((8, BLOCK), jnp.float32), jnp.zeros((width, BLOCK), jnp.float32)),
+    )
+    inverse = 1.0 / jnp.sum(total, 0, keepdims=True)
+    output = output * inverse
+    grad_wide = grad.astype(jnp.float32)
+    row_delta = jnp.sum(output * grad_wide.T, 0, keepdims=True)
+    column = jnp.broadcast_to(inverse, (width, BLOCK)).T
+    query_scaled = (query.astype(jnp.float32) * (column * scaling)).astype(jnp.bfloat16)
+    grad_scaled = (grad_wide * column).astype(jnp.bfloat16)
+
+    def backward_step(slot, grad_query):
+        index = block_of(slot)
+        values = value_ref[index >> inner_bits, 0, index & inner_mask]
+        weights = weight_ref[slot]
+        grad_weights = product(values, grad, NT)
+        grad_logits = (weights.astype(jnp.float32) * (grad_weights - row_delta)).astype(
+            jnp.bfloat16
+        )
+        key_sum[index] += product(grad_logits, query_scaled, NN)
+        value_sum[index] += product(weights, grad_scaled, NN)
+        return grad_query + product(key_flip[index], grad_logits, NN)
+
+    grad_query = over_slots(backward_step, jnp.zeros((width, BLOCK), jnp.float32))
+    grad_query = grad_query * (inverse * scaling)
+    major, minor = block >> inner_bits, block & inner_mask
+    out_ref[major, 0, minor] = output.T.astype(jnp.bfloat16)
+    out_ref[major, 1, minor] = grad_query.T.astype(jnp.bfloat16)
+
+    @pl.when(block == total_blocks - 1)
+    def _():
+        def finish(index, carry):
+            major, minor = index >> inner_bits, index & inner_mask
+            out_ref[major, 2, minor] = key_sum[index].astype(jnp.bfloat16)
+            out_ref[major, 3, minor] = value_sum[index].astype(jnp.bfloat16)
+            return carry
+
+        lax.fori_loop(0, total_blocks, finish, 0)
+
+
+def head_attention(packed, global_blocks):
+    seq_count, _, block_count, _, width = packed.shape
+    total_blocks = seq_count * block_count
+    level_count = total_blocks.bit_length() - 1
+    inner_bits = block_count.bit_length() - 1
+    slot_count = 1 + level_count + global_blocks.shape[0]
+    inner_mask = block_count - 1
+
+    def one(array):
+        return pl.BlockSpec(
+            (1, 1, 1, BLOCK, width),
+            lambda block: (block >> inner_bits, array, block & inner_mask, 0, 0),
+        )
+
+    def whole(array):
+        return pl.BlockSpec(
+            (seq_count, 1, block_count, BLOCK, width), lambda block: (0, array, 0, 0, 0)
+        )
+
+    pairs = total_blocks * slot_count * BLOCK * BLOCK
+    return pl.pallas_call(
+        functools.partial(head_kernel, level_count, inner_bits, 1.0 / math.sqrt(width)),
+        grid=(total_blocks,),
+        out_shape=jax.ShapeDtypeStruct(packed.shape, jnp.bfloat16),
+        in_specs=[pl.BlockSpec(memory_space=pltpu.SMEM), one(0), one(3), whole(1), whole(2)],
+        out_specs=pl.BlockSpec(packed.shape, lambda block: (0, 0, 0, 0, 0)),
+        scratch_shapes=[
+            pltpu.VMEM((total_blocks, width, BLOCK), jnp.bfloat16),
+            pltpu.VMEM((total_blocks, width, BLOCK), jnp.bfloat16),
+            pltpu.VMEM((total_blocks, BLOCK, width), jnp.float32),
+            pltpu.VMEM((total_blocks, BLOCK, width), jnp.float32),
+            pltpu.VMEM((slot_count, BLOCK, BLOCK), jnp.float32),
+            pltpu.VMEM((slot_count, BLOCK, BLOCK), jnp.bfloat16),
+            pltpu.SMEM((global_blocks.shape[0],), jnp.int32),
+        ],
+        compiler_params=pltpu.CompilerParams(
+            dimension_semantics=("arbitrary",), vmem_limit_bytes=48 * 1024 * 1024
+        ),
+        cost_estimate=pl.CostEstimate(
+            flops=12 * pairs * width, bytes_accessed=4 * packed.size, transcendentals=pairs
+        ),
+    )(global_blocks, packed, packed, packed, packed)
+
+
+def head_plan(queries, key_rows, value_rows, grad_out, global_blocks):
+    row_count, head_count, head_width = queries.shape
+    packed = jnp.stack(
+        [array.transpose(1, 0, 2) for array in (queries, key_rows, value_rows, grad_out)], 1
+    )
+    packed = lax.all_to_all(packed, "seq", split_axis=0, concat_axis=0, tiled=True)
+    packed = packed.reshape(head_count, 4, row_count // BLOCK, BLOCK, head_width)
+    result = head_attention(packed, global_blocks)
+    result = result.reshape(head_count, 4, row_count, head_width)
+    result = lax.all_to_all(result, "seq", split_axis=0, concat_axis=0, tiled=True)
+    return tuple(result[:, index].transpose(1, 0, 2) for index in range(4))
+
+
+def on_device(*operands):
+    one_head_each = operands[0].shape[1] == lax.axis_size("seq")
+    return (head_plan if one_head_each else gathered_plan)(*operands)
+
+
 def solution(mesh):
     in_specs = (
         P(("groups", "seq"), ("head", "sub"), None),

time: 993 us -> 287 us (0.29)
  waiting for transfers between devices: 519 us -> 0 us
  blocking collectives: 0 us -> 195 us
  local copies, waits for them, and re-layouts: 162 us -> 9.57 us
  matrix products: 125 us -> 0 us
  other arithmetic: 113 us -> 0.57 us
  Pallas kernels: 0 us -> 79 us
  between operations: 34.5 us -> 0.71 us
  starting transfers between devices: 31.3 us -> 0 us
    all_to_all x0 -> x2, blocking collectives: none -> 195 us  [the longest x1 98.4 us: head_plan(): lax.all_to_all(packed, 'seq', split_axis=0, concat_axis=0, tiled=True)]
    ppermute x12 -> x0, waiting for transfers between devices: 192 us -> none  [from_partner(): return lax.ppermute(value, axis, pairs)]
    psum x1 -> x0, waiting for transfers between devices: 165 us -> none  [spread(): return lax.psum(jnp.where(mine, array, jnp.zeros_like(array)), axis)]
    reduce_scatter x2 -> x0, waiting for transfers between devices: 147 us -> none  [the longest x1 92.4 us: on_device(): lax.psum_scatter(value_partial.astype(jnp.bfloat16), 'seq', scatter_dimen...]
    dot_general x12 -> x0, matrix products: 125 us -> none  [the longest x1 17.9 us: backward_group(): jnp.einsum('gqhd,nkhd->ghqnk', grad_group, global_values, preferred_eleme...]
    convert_element_type x7 -> x0, other arithmetic: 80.2 us -> none  [the longest x1 43.6 us: backward_group(): (weights * (grad_weights - row_delta[..., None]) * scaling).astype(jnp.bf...]
    pallas_call x0 -> x1, Pallas kernels: none -> 79 us  [head_attention(): pl.pallas_call(functools.partial(head_kernel, level_count, inner_bits, 1....]
    slice x5 -> x0, local copies, waits for them, and re-layouts: 47.3 us -> none  [the longest x2 27.8 us: split_keys(): array[..., slot_count * block_rows:].reshape(lead_shape + (-1, block_rows))]
  transfers between devices with their start and end apart: 17 -> 0, of which waited for: 11 -> 0; matrix products, arithmetic and copies ran while one was open for 13% -> 0% of each run, Pallas kernels for 0% -> 0%
where the time goes in v1:
time: 287 us; the launch traced here: 284 us
  blocking collectives  195 us (68%)
  Pallas kernels  79 us (28%)
  local copies, waits for them, and re-layouts  9.57 us (3%)
    all_to_all x1, blocking collectives, head_plan(): lax.all_to_all(packed, 'seq', split_axis=0, concat_axis=0, tiled=True)  98.4 us
    all_to_all x1, blocking collectives, head_plan(): lax.all_to_all(result, 'seq', split_axis=0, concat_axis=0, tiled=True)  96.2 us
    pallas_call x1, Pallas kernels, head_attention(): pl.pallas_call(functools.partial(head_kernel, level_count, inner_bits, 1....  79 us
    unnamed x10, local copies, waits for them, and re-layouts  6.68 us

profile of v1, /device:TPU:8, one launch (start us, length us, event | category | flops | bytes accessed | tf_op | source)
XLA Modules:
  0.0 284.4 jit_solution(1666050633556012424)
XLA Ops:
  0.6 0.0 copy-start.1
  0.6 0.0 copy-start.2
  0.7 2.1 copy_bitcast_fusion.2
  2.7 0.0 copy-done.1
  2.7 0.1 copy-done.2
  2.8 0.4 copy_bitcast_fusion
  3.2 0.6 pad_maximum_fusion
  3.8 0.0 copy-start
  3.8 98.4 %all_to_all.10 = bf16[8,4,512,128]{3,2,1,0:T(8,128)(2,1)} all-to-all(bf16[8,4,512,128]{3,2,1,0:T(8,128)(2,1)S(1)} %pad_maximum_fusion), channel_id=1, replica_groups=mesh['groups'=2,'seq'=8,'head'=1,'sub'=2] {'seq'}, dimensions={0} | all-to-all | bytes 8388608 | tf_op jit(solution)/shard_map/all_to_all | solution.py:442
  102.2 0.0 copy-done
  102.2 79.0 %shard_map.84 = bf16[8,4,2,256,128]{4,3,2,1,0:T(8,128)(2,1)S(1)} custom-call(s32[8]{0:T(128)S(1)} %copy-done, bf16[8,4,2,256,128]{4,3,2,1,0:T(8,128)(2,1)} %bitcast.35, bf16[8,4,2,256,128]{4,3,2,1,0:T(8,128)(2,1)} %bitcast.36, bf16[8,4,2,256,128]{4,3,2,1,0:T(8,128)(2,1)} %bitcast.37, bf16[8,4,2,256,128]{4,3,2,1,0:T(8,128)(2,1)} %bitcast.38), custom_call_target="tpu_custom_call" | custom-call | flops 20937965568 | bytes 8388608 | tf_op jit(solution)/shard_map/pallas_call | solution.py:413
  181.2 96.2 %all_to_all.11 = bf16[8,4,512,128]{3,2,1,0:T(8,128)(2,1)S(1)} all-to-all(bf16[8,4,512,128]{3,2,1,0:T(8,128)(2,1)S(1)} %bitcast.34), channel_id=1, replica_groups=mesh['groups'=2,'seq'=8,'head'=1,'sub'=2] {'seq'}, dimensions={0} | all-to-all | bytes 8388608 | tf_op jit(solution)/shard_map/all_to_all | solution.py:446
  277.4 0.4 slice_bitcast_fusion
  277.8 1.7 copy.18
  279.5 1.6 copy.17
  281.1 1.6 copy.16
  282.8 1.6 copy.15
Async XLA Ops:
  0.6 2.1 copy-start.1
  0.6 2.2 copy-start.2
  3.8 98.4 %copy-start = (s32[8]{0:T(128)S(1)}, s32[8]{0:T(128)}, u32[]{:S(2)}) copy-start(s32[8]{0:T(128)} %globals_ref.1) | copy-start | bytes 100

commit v2 on v1

--- a/solution.py
+++ b/solution.py
@@ -273,21 +273,26 @@
     level_count,
     inner_bits,
     scaling,
+    start,
+    finish,
+    source_count,
     globals_ref,
-    query_ref,
-    grad_ref,
     key_ref,
     value_ref,
-    out_ref,
-    key_flip,
-    value_flip,
-    key_sum,
-    value_sum,
-    logit_ref,
-    weight_ref,
-    table_ref,
+    *refs,
 ):
-    block = pl.program_id(0)
+    sources, refs = refs[:source_count], refs[source_count:]
+    if start == 0:
+        out_ref, key_flip, value_flip, *refs = refs
+    else:
+        key_flip, value_flip, key_carry, value_carry, out_ref, *refs = refs
+    if finish:
+        total_ref, *refs = refs
+    else:
+        key_out, value_out, *refs = refs
+    key_sum, value_sum, logit_ref, weight_ref, table_ref = refs
+    step = pl.program_id(0)
+    block = step + start
     total_blocks = key_flip.shape[0]
     width = key_flip.shape[1]
     inner_mask = (1 << inner_bits) - 1
@@ -295,16 +300,19 @@
     global_count = globals_ref.shape[0]
     factor = scaling * math.log2(math.e)
 
-    @pl.when(block == 0)
+    @pl.when(step == 0)
     def _():
         def prepare(index, carry):
             major, minor = index >> inner_bits, index & inner_mask
-            key_flip[index] = key_ref[major, 0, minor].astype(jnp.float32).T.astype(jnp.bfloat16)
-            value_flip[index] = (
-                value_ref[major, 0, minor].astype(jnp.float32).T.astype(jnp.bfloat16)
-            )
-            key_sum[index] = jnp.zeros((BLOCK, width), jnp.float32)
-            value_sum[index] = jnp.zeros((BLOCK, width), jnp.float32)
+            if start:
+                key_sum[index] = key_carry[index]
+                value_sum[index] = value_carry[index]
+            else:
+                keys, values = key_ref[major, 0, minor], value_ref[major, 0, minor]
+                key_flip[index] = keys.astype(jnp.float32).T.astype(jnp.bfloat16)
+                value_flip[index] = values.astype(jnp.float32).T.astype(jnp.bfloat16)
+                key_sum[index] = jnp.zeros((BLOCK, width), jnp.float32)
+                value_sum[index] = jnp.zeros((BLOCK, width), jnp.float32)
             return carry
 
         lax.fori_loop(0, total_blocks, prepare, 0)
@@ -328,8 +336,12 @@
             carry = body(slot, carry)
         return lax.fori_loop(fixed_count, slot_total, body, carry)
 
-    query = query_ref[0, 0, 0]
-    grad = grad_ref[0, 0, 0]
+    source, member = step >> inner_bits, step & inner_mask
+    query, grad = sources[0][0, member], sources[0][1, member]
+    for place in range(1, source_count):
+        here = source == place
+        query = jnp.where(here, sources[place][0, member], query)
+        grad = jnp.where(here, sources[place][1, member], grad)
 
     def logits_step(slot, peak):
         index = block_of(slot)
@@ -375,80 +387,167 @@
 
     grad_query = over_slots(backward_step, jnp.zeros((width, BLOCK), jnp.float32))
     grad_query = grad_query * (inverse * scaling)
-    major, minor = block >> inner_bits, block & inner_mask
-    out_ref[major, 0, minor] = output.T.astype(jnp.bfloat16)
-    out_ref[major, 1, minor] = grad_query.T.astype(jnp.bfloat16)
-
-    @pl.when(block == total_blocks - 1)
+    out_ref[0, 0, 0] = output.T.astype(jnp.bfloat16)
+    out_ref[0, 1, 0] = grad_query.T.astype(jnp.bfloat16)
+
+    @pl.when(step == pl.num_programs(0) - 1)
     def _():
-        def finish(index, carry):
-            major, minor = index >> inner_bits, index & inner_mask
-            out_ref[major, 2, minor] = key_sum[index].astype(jnp.bfloat16)
-            out_ref[major, 3, minor] = value_sum[index].astype(jnp.bfloat16)
+        def hand_on(index, carry):
+            if finish:
+                major, minor = index >> inner_bits, index & inner_mask
+                total_ref[major, 0, minor] = key_sum[index].astype(jnp.bfloat16)
+                total_ref[major, 1, minor] = value_sum[index].astype(jnp.bfloat16)
+            else:
+                key_out[index] = key_sum[index]
+                value_out[index] = value_sum[index]
             return carry
 
-        lax.fori_loop(0, total_blocks, finish, 0)
-
-
-def head_attention(packed, global_blocks):
-    seq_count, _, block_count, _, width = packed.shape
+        lax.fori_loop(0, total_blocks, hand_on, 0)
+
+
+def head_attention(query_parts, key_pack, global_blocks, state, start, finish):
+    seq_count, _, block_count, _, width = key_pack.shape
     total_blocks = seq_count * block_count
     level_count = total_blocks.bit_length() - 1
     inner_bits = block_count.bit_length() - 1
     slot_count = 1 + level_count + global_blocks.shape[0]
     inner_mask = block_count - 1
-
-    def one(array):
+    steps = len(query_parts) * block_count
+
+    def half(array):
         return pl.BlockSpec(
-            (1, 1, 1, BLOCK, width),
-            lambda block: (block >> inner_bits, array, block & inner_mask, 0, 0),
-        )
-
-    def whole(array):
+            (seq_count, 1, block_count, BLOCK, width),
+            lambda step: (0, array, 0, 0, 0),
+            pipeline_mode=pl.Buffered(1),
+        )
+
+    def whole(shape):
         return pl.BlockSpec(
-            (seq_count, 1, block_count, BLOCK, width), lambda block: (0, array, 0, 0, 0)
-        )
-
-    pairs = total_blocks * slot_count * BLOCK * BLOCK
+            shape, lambda step: (0,) * len(shape), pipeline_mode=pl.Buffered(1)
+        )
+
+    flip_shape = (total_blocks, width, BLOCK)
+    sum_shape = (total_blocks, BLOCK, width)
+    in_specs = [pl.BlockSpec(memory_space=pltpu.SMEM), half(0), half(1)]
+    in_specs += [whole(part.shape) for part in query_parts]
+    out_shape = [jax.ShapeDtypeStruct((len(query_parts),) + key_pack.shape[1:], jnp.bfloat16)]
+    out_specs = [
+        pl.BlockSpec(
+            (1, 2, 1, BLOCK, width), lambda step: (step >> inner_bits, 0, step & inner_mask, 0, 0)
+        )
+    ]
+    if start == 0:
+        out_shape += [jax.ShapeDtypeStruct(flip_shape, jnp.bfloat16)] * 2
+        out_specs += [whole(flip_shape)] * 2
+    else:
+        in_specs += [whole(flip_shape)] * 2 + [whole(sum_shape)] * 2
+    if finish:
+        out_shape += [jax.ShapeDtypeStruct(key_pack.shape, jnp.bfloat16)]
+        out_specs += [whole(key_pack.shape)]
+    else:
+        out_shape += [jax.ShapeDtypeStruct(sum_shape, jnp.float32)] * 2
+        out_specs += [whole(sum_shape)] * 2
+    pairs = steps * slot_count * BLOCK * BLOCK
     return pl.pallas_call(
-        functools.partial(head_kernel, level_count, inner_bits, 1.0 / math.sqrt(width)),
-        grid=(total_blocks,),
-        out_shape=jax.ShapeDtypeStruct(packed.shape, jnp.bfloat16),
-        in_specs=[pl.BlockSpec(memory_space=pltpu.SMEM), one(0), one(3), whole(1), whole(2)],
-        out_specs=pl.BlockSpec(packed.shape, lambda block: (0, 0, 0, 0, 0)),
+        functools.partial(
+            head_kernel,
+            level_count,
+            inner_bits,
+            1.0 / math.sqrt(width),
+            start * block_count,
+            finish,
+            len(query_parts),
+        ),
+        grid=(steps,),
+        out_shape=out_shape,
+        in_specs=in_specs,
+        out_specs=out_specs,
         scratch_shapes=[
-            pltpu.VMEM((total_blocks, width, BLOCK), jnp.bfloat16),
-            pltpu.VMEM((total_blocks, width, BLOCK), jnp.bfloat16),
-            pltpu.VMEM((total_blocks, BLOCK, width), jnp.float32),
-            pltpu.VMEM((total_blocks, BLOCK, width), jnp.float32),
+            pltpu.VMEM(sum_shape, jnp.float32),
+            pltpu.VMEM(sum_shape, jnp.float32),
             pltpu.VMEM((slot_count, BLOCK, BLOCK), jnp.float32),
             pltpu.VMEM((slot_count, BLOCK, BLOCK), jnp.bfloat16),
             pltpu.SMEM((global_blocks.shape[0],), jnp.int32),
         ],
         compiler_params=pltpu.CompilerParams(
-            dimension_semantics=("arbitrary",), vmem_limit_bytes=48 * 1024 * 1024
+            dimension_semantics=("arbitrary",), vmem_limit_bytes=40 * 1024 * 1024
         ),
         cost_estimate=pl.CostEstimate(
-            flops=12 * pairs * width, bytes_accessed=4 * packed.size, transcendentals=pairs
+            flops=48 * pairs * width, bytes_accessed=8 * key_pack.size, transcendentals=pairs
         ),
-    )(global_blocks, packed, packed, packed, packed)
+    )(global_blocks, key_pack, key_pack, *query_parts, *state)
+
+
+def swap(array, distance):
+    pairs = [(source, source ^ distance) for source in range(lax.axis_size("seq"))]
+    return lax.ppermute(array, "seq", pairs) if distance else array
+
+
+def after(array, earlier):
+    return lax.optimization_barrier((array, earlier))[0]
 
 
 def head_plan(queries, key_rows, value_rows, grad_out, global_blocks):
     row_count, head_count, head_width = queries.shape
-    packed = jnp.stack(
-        [array.transpose(1, 0, 2) for array in (queries, key_rows, value_rows, grad_out)], 1
-    )
-    packed = lax.all_to_all(packed, "seq", split_axis=0, concat_axis=0, tiled=True)
-    packed = packed.reshape(head_count, 4, row_count // BLOCK, BLOCK, head_width)
-    result = head_attention(packed, global_blocks)
-    result = result.reshape(head_count, 4, row_count, head_width)
-    result = lax.all_to_all(result, "seq", split_axis=0, concat_axis=0, tiled=True)
-    return tuple(result[:, index].transpose(1, 0, 2) for index in range(4))
+    seq_count = lax.axis_size("seq")
+    block_count = row_count // BLOCK
+    me = lax.axis_index("seq")
+    pack_shape = (2, block_count, BLOCK, head_width)
+
+    def pack(first, second):
+        packed = jnp.stack([first.transpose(1, 0, 2), second.transpose(1, 0, 2)], 1)
+        packed = packed.reshape((head_count,) + pack_shape)
+        return [
+            lax.dynamic_index_in_dim(packed, me ^ distance, 0, keepdims=False)
+            for distance in range(seq_count)
+        ]
+
+    key_send = pack(key_rows, value_rows)
+    query_send = pack(queries, grad_out)
+    key_parts = [swap(key_send[distance], distance) for distance in range(seq_count)]
+    query_parts = [
+        swap(after(query_send[distance], key_parts[distance]), distance)
+        for distance in range(seq_count)
+    ]
+    key_pack = jnp.stack(key_parts, 0)
+    relabelled = global_blocks ^ (me * block_count)
+    bounds = [0, seq_count // 2, 3 * seq_count // 4, seq_count]
+    state = ()
+    query_back = []
+    for start, stop in zip(bounds[:-1], bounds[1:]):
+        finish = stop == seq_count
+        parts = query_parts[start:stop]
+        if finish:
+            parts = [after(part, query_back[1 : bounds[1]]) for part in parts]
+        out, *rest = head_attention(parts, key_pack, relabelled, state, start, finish)
+        if start == 0:
+            flips, rest = tuple(rest[:2]), rest[2:]
+        state = flips + tuple(rest)
+        query_back += [swap(out[distance - start], distance) for distance in range(start, stop)]
+    totals = rest[0]
+    middle = query_back[bounds[1] : bounds[2]]
+    key_back = [
+        swap(after(totals[distance], middle) if distance else totals[distance], distance)
+        for distance in range(seq_count)
+    ]
+
+    def unpack(parts):
+        stacked = jnp.stack(parts, 0)
+        ordered = jnp.stack(
+            [
+                lax.dynamic_index_in_dim(stacked, me ^ head, 0, keepdims=False)
+                for head in range(head_count)
+            ],
+            0,
+        ).reshape(head_count, 2, row_count, head_width)
+        return (ordered[:, 0].transpose(1, 0, 2), ordered[:, 1].transpose(1, 0, 2))
+
+    return unpack(query_back) + unpack(key_back)
 
 
 def on_device(*operands):
-    one_head_each = operands[0].shape[1] == lax.axis_size("seq")
+    seq_count = lax.axis_size("seq")
+    one_head_each = operands[0].shape[1] == seq_count and seq_count % 4 == 0
     return (head_plan if one_head_each else gathered_plan)(*operands)
 
 

time: 287 us -> 244 us (0.85)
  blocking collectives: 195 us -> 0 us
  waiting for transfers between devices: 0 us -> 97 us
  starting transfers between devices: 0 us -> 40 us
  local copies, waits for them, and re-layouts: 9.57 us -> 19.4 us
    all_to_all x2 -> x0, blocking collectives: 195 us -> none  [the longest x1 98.4 us: head_plan(): lax.all_to_all(packed, 'seq', split_axis=0, concat_axis=0, tiled=True)]
    ppermute x0 -> x28, waiting for transfers between devices: none -> 97 us  [swap(): return lax.ppermute(array, 'seq', pairs) if distance else array]
    ppermute x0 -> x28, starting transfers between devices: none -> 40 us  [swap(): return lax.ppermute(array, 'seq', pairs) if distance else array]
    unnamed x10 -> x49, local copies, waits for them, and re-layouts: 6.68 us -> 15.7 us
    squeeze x0 -> x2, other arithmetic: none -> 3.2 us  [pack(): lax.dynamic_index_in_dim(packed, me ^ distance, 0, keepdims=False)]
    pallas_call x1 -> x3, Pallas kernels: 79 us -> 80.3 us  [head_attention(): pl.pallas_call(functools.partial(head_kernel, level_count, inner_bits, 1....]
  transfers between devices with their start and end apart: 0 -> 28, of which waited for: 0 -> 10; matrix products, arithmetic and copies ran while one was open for 0% -> 5% of each run, Pallas kernels for 0% -> 33%
where the time goes in v2:
time: 244 us; the launch traced here: 241 us
  waiting for transfers between devices  97 us (40%)
  Pallas kernels  80.3 us (33%)
  starting transfers between devices  40 us (16%)
  local copies, waits for them, and re-layouts  19.4 us (8%)
  other arithmetic  3.21 us (1%)
    ppermute x28, waiting for transfers between devices, swap(): return lax.ppermute(array, 'seq', pairs) if distance else array  97 us
    pallas_call x3, Pallas kernels, head_attention(): pl.pallas_call(functools.partial(head_kernel, level_count, inner_bits, 1....  80.3 us
    ppermute x28, starting transfers between devices, swap(): return lax.ppermute(array, 'seq', pairs) if distance else array  40 us
    unnamed x49, local copies, waits for them, and re-layouts  15.7 us
  transfers between devices with their start and end apart: 28, of which 10 were waited for; matrix products, arithmetic and copies ran while one was open for 5% of the time, Pallas kernels for 33%

profile of v2, /device:TPU:8, one launch (start us, length us, event | category | flops | bytes accessed | tf_op | source)
XLA Modules:
  0.0 241.0 jit_solution(17508887537869827494)
XLA Ops:
  4.8 2.2 collective-permute-start.4
  7.0 2.3 fusion.15
  9.3 2.7 %collective-permute-start.6 = (bf16[2,2,256,128]{3,2,1,0:T(8,128)(2,1)S(1)}, bf16[2,2,256,128]{3,2,1,0:T(8,128)(2,1)S(1)}, u32[]{:S(2)}, u32[]{:S(2)}) collective-permute-start(bf16[2,2,256,128]{3,2,1,0:T(8,128)(2,1)S(1)} %get-tuple-element.76), channel_id=1, source_target_pairs={{0,14},{2,12},{4,10},{6,8},{8,6},{10,4},{12,2},{14,0},{1,15},{3,13... | collective-permute-start | bytes 786440 | tf_op jit(solution)/shard_map/ppermute | solution.py:483
  15.6 13.6 %collective-permute-done.5 = bf16[2,2,256,128]{3,2,1,0:T(8,128)(2,1)} collective-permute-done((bf16[2,2,256,128]{3,2,1,0:T(8,128)(2,1)S(1)}, bf16[2,2,256,128]{3,2,1,0:T(8,128)(2,1)}, u32[]{:S(2)}, u32[]{:S(2)}) %collective-permute-start.5) | collective-permute-done | bytes 262176 | tf_op jit(solution)/shard_map/ppermute | solution.py:483
  29.2 13.3 %collective-permute-done.6 = bf16[2,2,256,128]{3,2,1,0:T(8,128)(2,1)S(1)} collective-permute-done((bf16[2,2,256,128]{3,2,1,0:T(8,128)(2,1)S(1)}, bf16[2,2,256,128]{3,2,1,0:T(8,128)(2,1)S(1)}, u32[]{:S(2)}, u32[]{:S(2)}) %collective-permute-start.6) | collective-permute-done | bytes 262176 | tf_op jit(solution)/shard_map/ppermute | solution.py:483
  44.2 10.0 %collective-permute-done.3 = bf16[2,2,256,128]{3,2,1,0:T(8,128)(2,1)} collective-permute-done((bf16[2,2,256,128]{3,2,1,0:T(8,128)(2,1)}, bf16[2,2,256,128]{3,2,1,0:T(8,128)(2,1)}, u32[]{:S(2)}, u32[]{:S(2)}) %collective-permute-start.3) | collective-permute-done | bytes 262176 | tf_op jit(solution)/shard_map/ppermute | solution.py:483
  55.7 3.1 %collective-permute-start.8 = (bf16[2,2,256,128]{3,2,1,0:T(8,128)(2,1)}, bf16[2,2,256,128]{3,2,1,0:T(8,128)(2,1)S(1)}, u32[]{:S(2)}, u32[]{:S(2)}) collective-permute-start(bf16[2,2,256,128]{3,2,1,0:T(8,128)(2,1)} %get-tuple-element.31), channel_id=1, source_target_pairs={{0,4},{2,6},{4,0},{6,2},{8,12},{10,14},{12,8},{14,10},{1,5},{3,7},... | collective-permute-start | bytes 786440 | tf_op jit(solution)/shard_map/ppermute | solution.py:483
  58.8 2.3 collective-permute-start.13
  69.5 4.4 %collective-permute-done.8.refs_2_ = bf16[2,2,256,128]{3,2,1,0:T(8,128)(2,1)S(1)} collective-permute-done((bf16[2,2,256,128]{3,2,1,0:T(8,128)(2,1)}, bf16[2,2,256,128]{3,2,1,0:T(8,128)(2,1)S(1)}, u32[]{:S(2)}, u32[]{:S(2)}) %collective-permute-start.8) | collective-permute-done | bytes 262176 | tf_op jit(solution)/shard_map/ppermute | solution.py:483
  75.0 2.1 collective-permute-done.9.refs_3_
  77.1 40.2 %shard_map.84 = (bf16[4,2,2,256,128]{4,3,2,1,0:T(8,128)(2,1)S(1)}, bf16[16,128,256]{2,1,0:T(8,128)(2,1)S(1)}, bf16[16,128,256]{2,1,0:T(8,128)(2,1)S(1)}, f32[16,256,128]{2,1,0:T(8,128)S(1)}, f32[16,256,128]{2,1,0:T(8,128)S(1)}) custom-call(s32[8]{0:T(128)S(1)} %broadcast_xor_fusion.globals_ref, ...), custom_call_target="tpu_custom_call" | custom-call | flops 41875931136 | bytes 8388608 | tf_op jit(solution)/shard_map/pallas_call | solution.py:451
  117.4 3.3 %collective-permute-start.12 = (bf16[2,2,256,128]{3,2,1,0:T(8,128)(2,1)S(1)}, bf16[2,2,256,128]{3,2,1,0:T(8,128)(2,1)S(1)}, u32[]{:S(2)}, u32[]{:S(2)}) collective-permute-start(bf16[2,2,256,128]{3,2,1,0:T(8,128)(2,1)S(1)} %get-tuple-element.84), channel_id=1, source_target_pairs={{0,6},{2,4},{4,2},{6,0},{8,14},{10,12},{12,10},{14,8},{1,7},{3,5},... | collective-permute-start | bytes 786440 | tf_op jit(solution)/shard_map/ppermute | solution.py:483
  121.4 20.7 %shard_map.85 = (bf16[2,2,2,256,128]{4,3,2,1,0:T(8,128)(2,1)S(1)}, f32[16,256,128]{2,1,0:T(8,128)S(1)}, f32[16,256,128]{2,1,0:T(8,128)S(1)}) custom-call(s32[8]{0:T(128)S(1)} %broadcast_xor_fusion.globals_ref, bf16[8,2,2,256,128]{4,3,2,1,0:T(8,128)(2,1)S(1)} %bitcast_dynamic-update-slice_fusion.14.key_ref.value_ref, ...), custom_call_target="tpu_custom_call" | custom-call | flops 20937965568 | bytes 8388608 | tf_op jit(solution)/shard_map/pallas_call | solution.py:451
  142.2 4.1 %collective-permute-start.16 = (bf16[2,2,256,128]{3,2,1,0:T(8,128)(2,1)S(1)}, bf16[2,2,256,128]{3,2,1,0:T(8,128)(2,1)S(1)}, u32[]{:S(2)}, u32[]{:S(2)}) collective-permute-start(bf16[2,2,256,128]{3,2,1,0:T(8,128)(2,1)S(1)} %get-tuple-element.90), channel_id=1, source_target_pairs={{0,10},{2,8},{4,14},{6,12},{8,2},{10,0},{12,6},{14,4},{1,11},{3,9}... | collective-permute-start | bytes 786440 | tf_op jit(solution)/shard_map/ppermute | solution.py:483
  146.3 19.3 %shard_map.86 = (bf16[2,2,2,256,128]{4,3,2,1,0:T(8,128)(2,1)S(1)}, bf16[8,2,2,256,128]{4,3,2,1,0:T(8,128)(2,1)S(1)}) custom-call(s32[8]{0:T(128)S(1)} %broadcast_xor_fusion.globals_ref, bf16[8,2,2,256,128]{4,3,2,1,0:T(8,128)(2,1)S(1)} %bitcast_dynamic-update-slice_fusion.14.key_ref.value_ref, ...), custom_call_target="tpu_custom_call" | custom-call | flops 20937965568 | bytes 8388608 | tf_op jit(solution)/shard_map/pallas_call | solution.py:451
  169.5 3.5 %collective-permute-start.22 = (bf16[2,2,256,128]{3,2,1,0:T(8,128)(2,1)S(1)}, bf16[2,2,256,128]{3,2,1,0:T(8,128)(2,1)S(1)}, u32[]{:S(2)}, u32[]{:S(2)}) collective-permute-start(bf16[2,2,256,128]{3,2,1,0:T(8,128)(2,1)S(1)} %get-tuple-element.50), channel_id=1, source_target_pairs={{0,4},{2,6},{4,0},{6,2},{8,12},{10,14},{12,8},{14,10},{1,5},{3,7},... | collective-permute-start | bytes 786440 | tf_op jit(solution)/shard_map/ppermute | solution.py:483
  173.3 14.2 %collective-permute-done.19 = bf16[2,2,256,128]{3,2,1,0:T(8,128)(2,1)S(1)} collective-permute-done((bf16[2,2,256,128]{3,2,1,0:T(8,128)(2,1)S(1)}, bf16[2,2,256,128]{3,2,1,0:T(8,128)(2,1)S(1)}, u32[]{:S(2)}, u32[]{:S(2)}) %collective-permute-start.19) | collective-permute-done | bytes 262176 | tf_op jit(solution)/shard_map/ppermute | solution.py:483
  187.5 3.8 %collective-permute-start.25 = (bf16[2,2,256,128]{3,2,1,0:T(8,128)(2,1)S(1)}, bf16[2,2,256,128]{3,2,1,0:T(8,128)(2,1)S(1)}, u32[]{:S(2)}, u32[]{:S(2)}) collective-permute-start(bf16[2,2,256,128]{3,2,1,0:T(8,128)(2,1)S(1)} %get-tuple-element.53), channel_id=1, source_target_pairs={{0,10},{2,8},{4,14},{6,12},{8,2},{10,0},{12,6},{14,4},{1,11},{3,9}... | collective-permute-start | bytes 786440 | tf_op jit(solution)/shard_map/ppermute | solution.py:483
  193.9 22.7 %collective-permute-done.24 = bf16[2,2,256,128]{3,2,1,0:T(8,128)(2,1)S(1)} collective-permute-done((bf16[2,2,256,128]{3,2,1,0:T(8,128)(2,1)S(1)}, bf16[2,2,256,128]{3,2,1,0:T(8,128)(2,1)S(1)}, u32[]{:S(2)}, u32[]{:S(2)}) %collective-permute-start.24) | collective-permute-done | bytes 262176 | tf_op jit(solution)/shard_map/ppermute | solution.py:483
  216.6 5.6 %collective-permute-done.25 = bf16[2,2,256,128]{3,2,1,0:T(8,128)(2,1)S(1)} collective-permute-done((bf16[2,2,256,128]{3,2,1,0:T(8,128)(2,1)S(1)}, bf16[2,2,256,128]{3,2,1,0:T(8,128)(2,1)S(1)}, u32[]{:S(2)}, u32[]{:S(2)}) %collective-permute-start.25) | collective-permute-done | bytes 262176 | tf_op jit(solution)/shard_map/ppermute | solution.py:483
  222.4 6.5 %collective-permute-done.26 = bf16[2,2,256,128]{3,2,1,0:T(8,128)(2,1)S(1)} collective-permute-done((bf16[2,2,256,128]{3,2,1,0:T(8,128)(2,1)S(1)}, bf16[2,2,256,128]{3,2,1,0:T(8,128)(2,1)S(1)}, u32[]{:S(2)}, u32[]{:S(2)}) %collective-permute-start.26) | collective-permute-done | bytes 262176 | tf_op jit(solution)/shard_map/ppermute | solution.py:483
  228.9 4.7 %collective-permute-done.27 = bf16[2,2,256,128]{3,2,1,0:T(8,128)(2,1)S(1)} collective-permute-done((bf16[2,2,256,128]{3,2,1,0:T(8,128)(2,1)S(1)}, bf16[2,2,256,128]{3,2,1,0:T(8,128)(2,1)S(1)}, u32[]{:S(2)}, u32[]{:S(2)}) %collective-permute-start.27) | collective-permute-done | bytes 262176 | tf_op jit(solution)/shard_map/ppermute | solution.py:483
  234.3 1.6 copy.29
  236.1 1.6 copy.27
  (101 shorter events, 32.0 us)
Async XLA Ops:
  3.2 26.0 %collective-permute-start.5 = (bf16[2,2,256,128]{3,2,1,0:T(8,128)(2,1)S(1)}, bf16[2,2,256,128]{3,2,1,0:T(8,128)(2,1)}, u32[]{:S(2)}, u32[]{:S(2)}) collective-permute-start(bf16[2,2,256,128]{3,2,1,0:T(8,128)(2,1)S(1)} %get-tuple-element.82), channel_id=1, source_target_pairs={{0,12},{2,14},{4,8},{6,10},{8,4},{10,6},{12,0},{14,2},{1,13},{3,15... | collective-permute-start | bytes 786440 | tf_op jit(solution)/shard_map/ppermute | solution.py:483
  4.8 39.4 %collective-permute-start.4 = (bf16[2,2,256,128]{3,2,1,0:T(8,128)(2,1)}, bf16[2,2,256,128]{3,2,1,0:T(8,128)(2,1)}, u32[]{:S(2)}, u32[]{:S(2)}) collective-permute-start(bf16[2,2,256,128]{3,2,1,0:T(8,128)(2,1)} %get-tuple-element.83), channel_id=1, source_target_pairs={{0,10},{2,8},{4,14},{6,12},{8,2},{10,0},{12,6},{14,4},{1,11},{3,9}... | collective-permute-start | bytes 786440 | tf_op jit(solution)/shard_map/ppermute | solution.py:483
  9.3 33.2 %collective-permute-start.6 = (bf16[2,2,256,128]{3,2,1,0:T(8,128)(2,1)S(1)}, bf16[2,2,256,128]{3,2,1,0:T(8,128)(2,1)S(1)}, u32[]{:S(2)}, u32[]{:S(2)}) collective-permute-start(bf16[2,2,256,128]{3,2,1,0:T(8,128)(2,1)S(1)} %get-tuple-element.76), channel_id=1, source_target_pairs={{0,14},{2,12},{4,10},{6,8},{8,6},{10,4},{12,2},{14,0},{1,15},{3,13... | collective-permute-start | bytes 786440 | tf_op jit(solution)/shard_map/ppermute | solution.py:483
  12.0 42.3 %collective-permute-start = (bf16[2,2,256,128]{3,2,1,0:T(8,128)(2,1)}, bf16[2,2,256,128]{3,2,1,0:T(8,128)(2,1)}, u32[]{:S(2)}, u32[]{:S(2)}) collective-permute-start(bf16[2,2,256,128]{3,2,1,0:T(8,128)(2,1)} %get-tuple-element.78), channel_id=1, source_target_pairs={{0,2},{2,0},{4,6},{6,4},{8,10},{10,8},{12,14},{14,12},{1,3},{3,1},... | collective-permute-start | bytes 786440 | tf_op jit(solution)/shard_map/ppermute | solution.py:483
  13.5 40.8 %collective-permute-start.1 = (bf16[2,2,256,128]{3,2,1,0:T(8,128)(2,1)}, bf16[2,2,256,128]{3,2,1,0:T(8,128)(2,1)}, u32[]{:S(2)}, u32[]{:S(2)}) collective-permute-start(bf16[2,2,256,128]{3,2,1,0:T(8,128)(2,1)} %get-tuple-element.79), channel_id=1, source_target_pairs={{0,4},{2,6},{4,0},{6,2},{8,12},{10,14},{12,8},{14,10},{1,5},{3,7},... | collective-permute-start | bytes 786440 | tf_op jit(solution)/shard_map/ppermute | solution.py:483
  29.2 25.0 %collective-permute-start.2 = (bf16[2,2,256,128]{3,2,1,0:T(8,128)(2,1)}, bf16[2,2,256,128]{3,2,1,0:T(8,128)(2,1)}, u32[]{:S(2)}, u32[]{:S(2)}) collective-permute-start(bf16[2,2,256,128]{3,2,1,0:T(8,128)(2,1)} %get-tuple-element.80), channel_id=1, source_target_pairs={{0,6},{2,4},{4,2},{6,0},{8,14},{10,12},{12,10},{14,8},{1,7},{3,5},... | collective-permute-start | bytes 786440 | tf_op jit(solution)/shard_map/ppermute | solution.py:483
  58.8 61.9 %collective-permute-start.13 = (bf16[2,2,256,128]{3,2,1,0:T(8,128)(2,1)S(1)}, bf16[2,2,256,128]{3,2,1,0:T(8,128)(2,1)S(1)}, u32[]{:S(2)}, u32[]{:S(2)}) collective-permute-start(bf16[2,2,256,128]{3,2,1,0:T(8,128)(2,1)S(1)} %get-tuple-element.34), channel_id=1, source_target_pairs={{0,8},{2,10},{4,12},{6,14},{8,0},{10,2},{12,4},{14,6},{1,9},{3,11}... | collective-permute-start | bytes 786440 | tf_op jit(solution)/shard_map/ppermute | solution.py:483
  61.2 59.6 %collective-permute-start.14 = (bf16[2,2,256,128]{3,2,1,0:T(8,128)(2,1)S(1)}, bf16[2,2,256,128]{3,2,1,0:T(8,128)(2,1)S(1)}, u32[]{:S(2)}, u32[]{:S(2)}) collective-permute-start(bf16[2,2,256,128]{3,2,1,0:T(8,128)(2,1)S(1)} %get-tuple-element.35), channel_id=1, source_target_pairs={{0,10},{2,8},{4,14},{6,12},{8,2},{10,0},{12,6},{14,4},{1,11},{3,9}... | collective-permute-start | bytes 786440 | tf_op jit(solution)/shard_map/ppermute | solution.py:483
  68.6 77.7 %collective-permute-start.17 = (bf16[2,2,256,128]{3,2,1,0:T(8,128)(2,1)S(1)}, bf16[2,2,256,128]{3,2,1,0:T(8,128)(2,1)S(1)}, u32[]{:S(2)}, u32[]{:S(2)}) collective-permute-start(bf16[2,2,256,128]{3,2,1,0:T(8,128)(2,1)S(1)} %get-tuple-element.41), channel_id=1, source_target_pairs={{0,12},{2,14},{4,8},{6,10},{8,4},{10,6},{12,0},{14,2},{1,13},{3,15... | collective-permute-start | bytes 786440 | tf_op jit(solution)/shard_map/ppermute | solution.py:483
  73.9 68.4 %collective-permute-start.18 = (bf16[2,2,256,128]{3,2,1,0:T(8,128)(2,1)S(1)}, bf16[2,2,256,128]{3,2,1,0:T(8,128)(2,1)S(1)}, u32[]{:S(2)}, u32[]{:S(2)}) collective-permute-start(bf16[2,2,256,128]{3,2,1,0:T(8,128)(2,1)S(1)} %get-tuple-element.43), channel_id=1, source_target_pairs={{0,14},{2,12},{4,10},{6,8},{8,6},{10,4},{12,2},{14,0},{1,15},{3,13... | collective-permute-start | bytes 786440 | tf_op jit(solution)/shard_map/ppermute | solution.py:483
  117.4 28.9 %collective-permute-start.12 = (bf16[2,2,256,128]{3,2,1,0:T(8,128)(2,1)S(1)}, bf16[2,2,256,128]{3,2,1,0:T(8,128)(2,1)S(1)}, u32[]{:S(2)}, u32[]{:S(2)}) collective-permute-start(bf16[2,2,256,128]{3,2,1,0:T(8,128)(2,1)S(1)} %get-tuple-element.84), channel_id=1, source_target_pairs={{0,6},{2,4},{4,2},{6,0},{8,14},{10,12},{12,10},{14,8},{1,7},{3,5},... | collective-permute-start | bytes 786440 | tf_op jit(solution)/shard_map/ppermute | solution.py:483
  120.8 25.5 %collective-permute-start.11 = (bf16[2,2,256,128]{3,2,1,0:T(8,128)(2,1)S(1)}, bf16[2,2,256,128]{3,2,1,0:T(8,128)(2,1)S(1)}, u32[]{:S(2)}, u32[]{:S(2)}) collective-permute-start(bf16[2,2,256,128]{3,2,1,0:T(8,128)(2,1)S(1)} %get-tuple-element.85), channel_id=1, source_target_pairs={{0,4},{2,6},{4,0},{6,2},{8,12},{10,14},{12,8},{14,10},{1,5},{3,7},... | collective-permute-start | bytes 786440 | tf_op jit(solution)/shard_map/ppermute | solution.py:483
  120.8 25.5 %collective-permute-start.10 = (bf16[2,2,256,128]{3,2,1,0:T(8,128)(2,1)S(1)}, bf16[2,2,256,128]{3,2,1,0:T(8,128)(2,1)S(1)}, u32[]{:S(2)}, u32[]{:S(2)}) collective-permute-start(bf16[2,2,256,128]{3,2,1,0:T(8,128)(2,1)S(1)} %get-tuple-element.86), channel_id=1, source_target_pairs={{0,2},{2,0},{4,6},{6,4},{8,10},{10,8},{12,14},{14,12},{1,3},{3,1},... | collective-permute-start | bytes 786440 | tf_op jit(solution)/shard_map/ppermute | solution.py:483
  142.2 25.8 %collective-permute-start.16 = (bf16[2,2,256,128]{3,2,1,0:T(8,128)(2,1)S(1)}, bf16[2,2,256,128]{3,2,1,0:T(8,128)(2,1)S(1)}, u32[]{:S(2)}, u32[]{:S(2)}) collective-permute-start(bf16[2,2,256,128]{3,2,1,0:T(8,128)(2,1)S(1)} %get-tuple-element.90), channel_id=1, source_target_pairs={{0,10},{2,8},{4,14},{6,12},{8,2},{10,0},{12,6},{14,4},{1,11},{3,9}... | collective-permute-start | bytes 786440 | tf_op jit(solution)/shard_map/ppermute | solution.py:483
  146.3 21.7 %collective-permute-start.15 = (bf16[2,2,256,128]{3,2,1,0:T(8,128)(2,1)S(1)}, bf16[2,2,256,128]{3,2,1,0:T(8,128)(2,1)S(1)}, u32[]{:S(2)}, u32[]{:S(2)}) collective-permute-start(bf16[2,2,256,128]{3,2,1,0:T(8,128)(2,1)S(1)} %get-tuple-element.91), channel_id=1, source_target_pairs={{0,8},{2,10},{4,12},{6,14},{8,0},{10,2},{12,4},{14,6},{1,9},{3,11}... | collective-permute-start | bytes 786440 | tf_op jit(solution)/shard_map/ppermute | solution.py:483
  165.7 21.8 %collective-permute-start.20 = (bf16[2,2,256,128]{3,2,1,0:T(8,128)(2,1)S(1)}, bf16[2,2,256,128]{3,2,1,0:T(8,128)(2,1)S(1)}, u32[]{:S(2)}, u32[]{:S(2)}) collective-permute-start(bf16[2,2,256,128]{3,2,1,0:T(8,128)(2,1)S(1)} %get-tuple-element.88), channel_id=1, source_target_pairs={{0,14},{2,12},{4,10},{6,8},{8,6},{10,4},{12,2},{14,0},{1,15},{3,13... | collective-permute-start | bytes 786440 | tf_op jit(solution)/shard_map/ppermute | solution.py:483
  166.9 20.5 %collective-permute-start.19 = (bf16[2,2,256,128]{3,2,1,0:T(8,128)(2,1)S(1)}, bf16[2,2,256,128]{3,2,1,0:T(8,128)(2,1)S(1)}, u32[]{:S(2)}, u32[]{:S(2)}) collective-permute-start(bf16[2,2,256,128]{3,2,1,0:T(8,128)(2,1)S(1)} %get-tuple-element.89), channel_id=1, source_target_pairs={{0,12},{2,14},{4,8},{6,10},{8,4},{10,6},{12,0},{14,2},{1,13},{3,15... | collective-permute-start | bytes 786440 | tf_op jit(solution)/shard_map/ppermute | solution.py:483
  168.0 23.3 %collective-permute-start.21 = (bf16[2,2,256,128]{3,2,1,0:T(8,128)(2,1)S(1)}, bf16[2,2,256,128]{3,2,1,0:T(8,128)(2,1)S(1)}, u32[]{:S(2)}, u32[]{:S(2)}) collective-permute-start(bf16[2,2,256,128]{3,2,1,0:T(8,128)(2,1)S(1)} %get-tuple-element.49), channel_id=1, source_target_pairs={{0,2},{2,0},{4,6},{6,4},{8,10},{10,8},{12,14},{14,12},{1,3},{3,1},... | collective-permute-start | bytes 786440 | tf_op jit(solution)/shard_map/ppermute | solution.py:483
  169.5 23.3 %collective-permute-start.22 = (bf16[2,2,256,128]{3,2,1,0:T(8,128)(2,1)S(1)}, bf16[2,2,256,128]{3,2,1,0:T(8,128)(2,1)S(1)}, u32[]{:S(2)}, u32[]{:S(2)}) collective-permute-start(bf16[2,2,256,128]{3,2,1,0:T(8,128)(2,1)S(1)} %get-tuple-element.50), channel_id=1, source_target_pairs={{0,4},{2,6},{4,0},{6,2},{8,12},{10,14},{12,8},{14,10},{1,5},{3,7},... | collective-permute-start | bytes 786440 | tf_op jit(solution)/shard_map/ppermute | solution.py:483
  173.0 20.7 %collective-permute-start.23 = (bf16[2,2,256,128]{3,2,1,0:T(8,128)(2,1)S(1)}, bf16[2,2,256,128]{3,2,1,0:T(8,128)(2,1)S(1)}, u32[]{:S(2)}, u32[]{:S(2)}) collective-permute-start(bf16[2,2,256,128]{3,2,1,0:T(8,128)(2,1)S(1)} %get-tuple-element.51), channel_id=1, source_target_pairs={{0,6},{2,4},{4,2},{6,0},{8,14},{10,12},{12,10},{14,8},{1,7},{3,5},... | collective-permute-start | bytes 786440 | tf_op jit(solution)/shard_map/ppermute | solution.py:483
  187.5 29.1 %collective-permute-start.24 = (bf16[2,2,256,128]{3,2,1,0:T(8,128)(2,1)S(1)}, bf16[2,2,256,128]{3,2,1,0:T(8,128)(2,1)S(1)}, u32[]{:S(2)}, u32[]{:S(2)}) collective-permute-start(bf16[2,2,256,128]{3,2,1,0:T(8,128)(2,1)S(1)} %get-tuple-element.52), channel_id=1, source_target_pairs={{0,8},{2,10},{4,12},{6,14},{8,0},{10,2},{12,4},{14,6},{1,9},{3,11}... | collective-permute-start | bytes 786440 | tf_op jit(solution)/shard_map/ppermute | solution.py:483
  187.5 34.7 %collective-permute-start.25 = (bf16[2,2,256,128]{3,2,1,0:T(8,128)(2,1)S(1)}, bf16[2,2,256,128]{3,2,1,0:T(8,128)(2,1)S(1)}, u32[]{:S(2)}, u32[]{:S(2)}) collective-permute-start(bf16[2,2,256,128]{3,2,1,0:T(8,128)(2,1)S(1)} %get-tuple-element.53), channel_id=1, source_target_pairs={{0,10},{2,8},{4,14},{6,12},{8,2},{10,0},{12,6},{14,4},{1,11},{3,9}... | collective-permute-start | bytes 786440 | tf_op jit(solution)/shard_map/ppermute | solution.py:483
  191.4 37.5 %collective-permute-start.26 = (bf16[2,2,256,128]{3,2,1,0:T(8,128)(2,1)S(1)}, bf16[2,2,256,128]{3,2,1,0:T(8,128)(2,1)S(1)}, u32[]{:S(2)}, u32[]{:S(2)}) collective-permute-start(bf16[2,2,256,128]{3,2,1,0:T(8,128)(2,1)S(1)} %get-tuple-element.54), channel_id=1, source_target_pairs={{0,12},{2,14},{4,8},{6,10},{8,4},{10,6},{12,0},{14,2},{1,13},{3,15... | collective-permute-start | bytes 786440 | tf_op jit(solution)/shard_map/ppermute | solution.py:483
  192.8 40.9 %collective-permute-start.27 = (bf16[2,2,256,128]{3,2,1,0:T(8,128)(2,1)S(1)}, bf16[2,2,256,128]{3,2,1,0:T(8,128)(2,1)S(1)}, u32[]{:S(2)}, u32[]{:S(2)}) collective-permute-start(bf16[2,2,256,128]{3,2,1,0:T(8,128)(2,1)S(1)} %get-tuple-element.55), channel_id=1, source_target_pairs={{0,14},{2,12},{4,10},{6,8},{8,6},{10,4},{12,2},{14,0},{1,15},{3,13... | collective-permute-start | bytes 786440 | tf_op jit(solution)/shard_map/ppermute | solution.py:483
  (10 other events, 102.6 us)

commit v3 on v2

--- a/solution.py
+++ b/solution.py
@@ -273,19 +273,19 @@
     level_count,
     inner_bits,
     scaling,
+    seq_count,
     start,
     finish,
     source_count,
     globals_ref,
-    key_ref,
-    value_ref,
     *refs,
 ):
     sources, refs = refs[:source_count], refs[source_count:]
     if start == 0:
-        out_ref, key_flip, value_flip, *refs = refs
+        key_parts, refs = refs[:seq_count], refs[seq_count:]
+        out_ref, key_ref, value_ref, key_flip, value_flip, *refs = refs
     else:
-        key_flip, value_flip, key_carry, value_carry, out_ref, *refs = refs
+        key_ref, value_ref, key_flip, value_flip, key_carry, value_carry, out_ref, *refs = refs
     if finish:
         total_ref, *refs = refs
     else:
@@ -302,15 +302,21 @@
 
     @pl.when(step == 0)
     def _():
+        if start == 0:
+            for place in range(seq_count):
+                for inner in range(inner_mask + 1):
+                    index = (place << inner_bits) + inner
+                    keys, values = key_parts[place][0, inner], key_parts[place][1, inner]
+                    key_ref[index] = keys
+                    value_ref[index] = values
+                    key_flip[index] = keys.astype(jnp.float32).T.astype(jnp.bfloat16)
+                    value_flip[index] = values.astype(jnp.float32).T.astype(jnp.bfloat16)
+
         def prepare(index, carry):
-            major, minor = index >> inner_bits, index & inner_mask
             if start:
                 key_sum[index] = key_carry[index]
                 value_sum[index] = value_carry[index]
             else:
-                keys, values = key_ref[major, 0, minor], value_ref[major, 0, minor]
-                key_flip[index] = keys.astype(jnp.float32).T.astype(jnp.bfloat16)
-                value_flip[index] = values.astype(jnp.float32).T.astype(jnp.bfloat16)
                 key_sum[index] = jnp.zeros((BLOCK, width), jnp.float32)
                 value_sum[index] = jnp.zeros((BLOCK, width), jnp.float32)
             return carry
@@ -345,7 +351,7 @@
 
     def logits_step(slot, peak):
         index = block_of(slot)
-        keys = key_ref[index >> inner_bits, 0, index & inner_mask]
+        keys = key_ref[index]
         logits = product(keys, query, NT)
         logit_ref[slot] = logits
         return jnp.maximum(peak, jnp.max(logits.reshape(BLOCK // 8, 8, BLOCK), 0))
@@ -375,7 +381,7 @@
 
     def backward_step(slot, grad_query):
         index = block_of(slot)
-        values = value_ref[index >> inner_bits, 0, index & inner_mask]
+        values = value_ref[index]
         weights = weight_ref[slot]
         grad_weights = product(values, grad, NT)
         grad_logits = (weights.astype(jnp.float32) * (grad_weights - row_delta)).astype(
@@ -405,8 +411,9 @@
         lax.fori_loop(0, total_blocks, hand_on, 0)
 
 
-def head_attention(query_parts, key_pack, global_blocks, state, start, finish):
-    seq_count, _, block_count, _, width = key_pack.shape
+def head_attention(query_parts, key_parts, global_blocks, state, seq_count, start, finish):
+    part_shape = query_parts[0].shape
+    _, block_count, _, width = part_shape
     total_blocks = seq_count * block_count
     level_count = total_blocks.bit_length() - 1
     inner_bits = block_count.bit_length() - 1
@@ -414,13 +421,6 @@
     inner_mask = block_count - 1
     steps = len(query_parts) * block_count
 
-    def half(array):
-        return pl.BlockSpec(
-            (seq_count, 1, block_count, BLOCK, width),
-            lambda step: (0, array, 0, 0, 0),
-            pipeline_mode=pl.Buffered(1),
-        )
-
     def whole(shape):
         return pl.BlockSpec(
             shape, lambda step: (0,) * len(shape), pipeline_mode=pl.Buffered(1)
@@ -428,22 +428,24 @@
 
     flip_shape = (total_blocks, width, BLOCK)
     sum_shape = (total_blocks, BLOCK, width)
-    in_specs = [pl.BlockSpec(memory_space=pltpu.SMEM), half(0), half(1)]
-    in_specs += [whole(part.shape) for part in query_parts]
-    out_shape = [jax.ShapeDtypeStruct((len(query_parts),) + key_pack.shape[1:], jnp.bfloat16)]
+    total_shape = (seq_count,) + part_shape
+    in_specs = [pl.BlockSpec(memory_space=pltpu.SMEM)]
+    in_specs += [whole(part_shape)] * (len(query_parts) + len(key_parts))
+    out_shape = [jax.ShapeDtypeStruct((len(query_parts),) + part_shape, jnp.bfloat16)]
     out_specs = [
         pl.BlockSpec(
             (1, 2, 1, BLOCK, width), lambda step: (step >> inner_bits, 0, step & inner_mask, 0, 0)
         )
     ]
     if start == 0:
+        out_shape += [jax.ShapeDtypeStruct(sum_shape, jnp.bfloat16)] * 2
         out_shape += [jax.ShapeDtypeStruct(flip_shape, jnp.bfloat16)] * 2
-        out_specs += [whole(flip_shape)] * 2
+        out_specs += [whole(sum_shape)] * 2 + [whole(flip_shape)] * 2
     else:
-        in_specs += [whole(flip_shape)] * 2 + [whole(sum_shape)] * 2
+        in_specs += [whole(sum_shape)] * 2 + [whole(flip_shape)] * 2 + [whole(sum_shape)] * 2
     if finish:
-        out_shape += [jax.ShapeDtypeStruct(key_pack.shape, jnp.bfloat16)]
-        out_specs += [whole(key_pack.shape)]
+        out_shape += [jax.ShapeDtypeStruct(total_shape, jnp.bfloat16)]
+        out_specs += [whole(total_shape)]
     else:
         out_shape += [jax.ShapeDtypeStruct(sum_shape, jnp.float32)] * 2
         out_specs += [whole(sum_shape)] * 2
@@ -454,6 +456,7 @@
             level_count,
             inner_bits,
             1.0 / math.sqrt(width),
+            seq_count,
             start * block_count,
             finish,
             len(query_parts),
@@ -473,9 +476,9 @@
             dimension_semantics=("arbitrary",), vmem_limit_bytes=40 * 1024 * 1024
         ),
         cost_estimate=pl.CostEstimate(
-            flops=48 * pairs * width, bytes_accessed=8 * key_pack.size, transcendentals=pairs
+            flops=48 * pairs * width, bytes_accessed=16 * total_blocks * BLOCK * width, transcendentals=pairs
         ),
-    )(global_blocks, key_pack, key_pack, *query_parts, *state)
+    )(global_blocks, *query_parts, *key_parts, *state)
 
 
 def swap(array, distance):
@@ -504,32 +507,53 @@
 
     key_send = pack(key_rows, value_rows)
     query_send = pack(queries, grad_out)
-    key_parts = [swap(key_send[distance], distance) for distance in range(seq_count)]
-    query_parts = [
-        swap(after(query_send[distance], key_parts[distance]), distance)
-        for distance in range(seq_count)
+    quarter = seq_count // 4
+    near, far = range(1, 2 * quarter), range(2 * quarter, seq_count)
+    key_parts, query_parts = [key_send[0]], [query_send[0]]
+    for distance in near:
+        key_parts.append(swap(after(key_send[distance], key_parts[-1]), distance))
+    key_parts += [swap(key_send[distance], distance) for distance in far]
+    earlier = key_parts[2 * quarter - 1]
+    for distance in near:
+        query_parts.append(swap(after(query_send[distance], earlier), distance))
+        earlier = query_parts[-1]
+    for distance in range(2 * quarter, 3 * quarter):
+        query_parts.append(swap(after(query_send[distance], key_parts[distance]), distance))
+    relabelled = global_blocks ^ (me * block_count)
+    state = ()
+    query_back = [None] * seq_count
+
+    def attend(start, earlier, finish=False):
+        parts = query_parts[start : start + quarter]
+        if earlier:
+            parts = [after(part, earlier) for part in parts]
+        out, *rest = head_attention(
+            parts, () if start else key_parts, relabelled, state, seq_count, start, finish
+        )
+        return out, rest
+
+    def give_back(start, out):
+        for distance in range(start, start + quarter):
+            query_back[distance] = swap(out[distance - start], distance)
+
+    out, rest = attend(0, None)
+    fixed, state = tuple(rest[:4]), tuple(rest)
+    give_back(0, out)
+    for distance in range(3 * quarter, seq_count):
+        query_parts.append(swap(after(query_send[distance], out), distance))
+    out, rest = attend(2 * quarter, None)
+    state = fixed + tuple(rest)
+    give_back(2 * quarter, out)
+    out, rest = attend(3 * quarter, query_back[1:quarter])
+    state = fixed + tuple(rest)
+    give_back(3 * quarter, out)
+    out, (totals,) = attend(quarter, query_back[2 * quarter : 3 * quarter], True)
+    last = query_back[3 * quarter :]
+    key_back = [totals[0]]
+    key_back += [
+        swap(after(totals[distance], last), distance) for distance in range(1, seq_count)
     ]
-    key_pack = jnp.stack(key_parts, 0)
-    relabelled = global_blocks ^ (me * block_count)
-    bounds = [0, seq_count // 2, 3 * seq_count // 4, seq_count]
-    state = ()
-    query_back = []
-    for start, stop in zip(bounds[:-1], bounds[1:]):
-        finish = stop == seq_count
-        parts = query_parts[start:stop]
-        if finish:
-            parts = [after(part, query_back[1 : bounds[1]]) for part in parts]
-        out, *rest = head_attention(parts, key_pack, relabelled, state, start, finish)
-        if start == 0:
-            flips, rest = tuple(rest[:2]), rest[2:]
-        state = flips + tuple(rest)
-        query_back += [swap(out[distance - start], distance) for distance in range(start, stop)]
-    totals = rest[0]
-    middle = query_back[bounds[1] : bounds[2]]
-    key_back = [
-        swap(after(totals[distance], middle) if distance else totals[distance], distance)
-        for distance in range(seq_count)
-    ]
+    give_back(quarter, after(out, key_back[1 : 1 + quarter]))
 
     def unpack(parts):
         stacked = jnp.stack(parts, 0)

time: 244 us -> 234 us (0.959)
  starting transfers between devices: 40 us -> 53.3 us
  waiting for transfers between devices: 97 us -> 85.7 us
  local copies, waits for them, and re-layouts: 19.4 us -> 11.7 us
  other arithmetic: 3.21 us -> 0.01 us
    ppermute x28, starting transfers between devices: 40 us -> 53.3 us  [swap(): return lax.ppermute(array, 'seq', pairs) if distance else array]
    unnamed x49 -> x36, local copies, waits for them, and re-layouts: 15.7 us -> 2.73 us
    ppermute x28, waiting for transfers between devices: 97 us -> 85.7 us  [swap(): return lax.ppermute(array, 'seq', pairs) if distance else array]
    transpose x2, local copies, waits for them, and re-layouts: 1.58 us -> 5.33 us  [unpack(): return (ordered[:, 0].transpose(1, 0, 2), ordered[:, 1].transpose(1, 0, 2))]
    squeeze x2 -> x0, other arithmetic: 3.2 us -> none  [pack(): lax.dynamic_index_in_dim(packed, me ^ distance, 0, keepdims=False)]
    pallas_call x3 -> x4, Pallas kernels: 80.3 us -> 80.3 us  [head_attention(): pl.pallas_call(functools.partial(head_kernel, level_count, inner_bits, 1....]
  transfers between devices with their start and end apart: 28 -> 28, of which waited for: 10 -> 12; matrix products, arithmetic and copies ran while one was open for 5% -> 2% of each run, Pallas kernels for 33% -> 35%
where the time goes in v3:
time: 234 us; the launch traced here: 232 us
  waiting for transfers between devices  85.7 us (37%)
  Pallas kernels  80.3 us (34%)
  starting transfers between devices  53.3 us (23%)
  local copies, waits for them, and re-layouts  11.7 us (5%)
    ppermute x28, waiting for transfers between devices, swap(): return lax.ppermute(array, 'seq', pairs) if distance else array  85.7 us
    pallas_call x4, Pallas kernels, head_attention(): pl.pallas_call(functools.partial(head_kernel, level_count, inner_bits, 1....  80.3 us
    ppermute x28, starting transfers between devices, swap(): return lax.ppermute(array, 'seq', pairs) if distance else array  53.3 us
    transpose x2, local copies, waits for them, and re-layouts, unpack(): return (ordered[:, 0].transpose(1, 0, 2), ordered[:, 1].transpose(1, 0, 2))  5.33 us
  transfers between devices with their start and end apart: 28, of which 12 were waited for; matrix products, arithmetic and copies ran while one was open for 2% of the time, Pallas kernels for 35%

profile of v3, /device:TPU:8, one launch (start us, length us, event | category | flops | bytes accessed | tf_op | source)
XLA Modules:
  0.0 232.1 jit_solution(2136922476917229607)
XLA Ops:
  8.0 9.3 %collective-permute-done.refs_3_ = bf16[2,2,256,128]{3,2,1,0:T(8,128)(2,1)S(1)} collective-permute-done((bf16[2,2,256,128]{3,2,1,0:T(8,128)(2,1)S(1)}, bf16[2,2,256,128]{3,2,1,0:T(8,128)(2,1)S(1)}, u32[]{:S(2)}, u32[]{:S(2)}) %collective-permute-start) | collective-permute-done | bytes 262176 | tf_op jit(solution)/shard_map/ppermute | solution.py:486
  17.5 14.6 %collective-permute-done.1.refs_4_ = bf16[2,2,256,128]{3,2,1,0:T(8,128)(2,1)S(1)} collective-permute-done((bf16[2,2,256,128]{3,2,1,0:T(8,128)(2,1)S(1)}, bf16[2,2,256,128]{3,2,1,0:T(8,128)(2,1)S(1)}, u32[]{:S(2)}, u32[]{:S(2)}) %collective-permute-start.1) | collective-permute-done | bytes 262176 | tf_op jit(solution)/shard_map/ppermute | solution.py:486
  32.1 3.7 %collective-permute-start.2 = (bf16[2,2,256,128]{3,2,1,0:T(8,128)(2,1)S(1)}, bf16[2,2,256,128]{3,2,1,0:T(8,128)(2,1)S(1)}, u32[]{:S(2)}, u32[]{:S(2)}) collective-permute-start(bf16[2,2,256,128]{3,2,1,0:T(8,128)(2,1)S(1)} %get-tuple-element.43), channel_id=1, source_target_pairs={{0,6},{2,4},{4,2},{6,0},{8,14},{10,12},{12,10},{14,8},{1,7},{3,5},... | collective-permute-start | bytes 786440 | tf_op jit(solution)/shard_map/ppermute | solution.py:486
  37.2 3.4 %collective-permute-done.2.refs_5_ = bf16[2,2,256,128]{3,2,1,0:T(8,128)(2,1)S(1)} collective-permute-done((bf16[2,2,256,128]{3,2,1,0:T(8,128)(2,1)S(1)}, bf16[2,2,256,128]{3,2,1,0:T(8,128)(2,1)S(1)}, u32[]{:S(2)}, u32[]{:S(2)}) %collective-permute-start.2) | collective-permute-done | bytes 262176 | tf_op jit(solution)/shard_map/ppermute | solution.py:486
  41.3 3.6 %collective-permute-start.7 = (bf16[2,2,256,128]{3,2,1,0:T(8,128)(2,1)}, bf16[2,2,256,128]{3,2,1,0:T(8,128)(2,1)S(1)}, u32[]{:S(2)}, u32[]{:S(2)}) collective-permute-start(bf16[2,2,256,128]{3,2,1,0:T(8,128)(2,1)} %get-tuple-element.98), channel_id=1, source_target_pairs={{0,14},{2,12},{4,10},{6,8},{8,6},{10,4},{12,2},{14,0},{1,15},{3,13... | collective-permute-start | bytes 786440 | tf_op jit(solution)/shard_map/ppermute | solution.py:486
  44.9 6.0 %collective-permute-start.11 = (bf16[2,2,256,128]{3,2,1,0:T(8,128)(2,1)}, bf16[2,2,256,128]{3,2,1,0:T(8,128)(2,1)S(1)}, u32[]{:S(2)}, u32[]{:S(2)}) collective-permute-start(bf16[2,2,256,128]{3,2,1,0:T(8,128)(2,1)} %get-tuple-element.48), channel_id=1, source_target_pairs={{0,10},{2,8},{4,14},{6,12},{8,2},{10,0},{12,6},{14,4},{1,11},{3,9}... | collective-permute-start | bytes 786440 | tf_op jit(solution)/shard_map/ppermute | solution.py:486
  53.0 20.2 %collective-permute-done.7.refs_9_ = bf16[2,2,256,128]{3,2,1,0:T(8,128)(2,1)S(1)} collective-permute-done((bf16[2,2,256,128]{3,2,1,0:T(8,128)(2,1)}, bf16[2,2,256,128]{3,2,1,0:T(8,128)(2,1)S(1)}, u32[]{:S(2)}, u32[]{:S(2)}) %collective-permute-start.7) | collective-permute-done | bytes 262176 | tf_op jit(solution)/shard_map/ppermute | solution.py:486
  73.2 5.1 %collective-permute-done.6.refs_8_ = bf16[2,2,256,128]{3,2,1,0:T(8,128)(2,1)S(1)} collective-permute-done((bf16[2,2,256,128]{3,2,1,0:T(8,128)(2,1)}, bf16[2,2,256,128]{3,2,1,0:T(8,128)(2,1)S(1)}, u32[]{:S(2)}, u32[]{:S(2)}) %collective-permute-start.6) | collective-permute-done | bytes 262176 | tf_op jit(solution)/shard_map/ppermute | solution.py:486
  78.4 18.9 %shard_map.84 = (bf16[2,2,2,256,128]{4,3,2,1,0:T(8,128)(2,1)S(1)}, bf16[16,256,128]{2,1,0:T(8,128)(2,1)S(1)}, bf16[16,256,128]{2,1,0:T(8,128)(2,1)S(1)}, bf16[16...) custom-call(s32[8]{0:T(128)S(1)} %broadcast_xor_fusion.globals_ref, ...), custom_call_target="tpu_custom_call" | custom-call | flops 20937965568 | bytes 8388608 | tf_op jit(solution)/shard_map/pallas_call | solution.py:453
  97.3 8.4 %collective-permute-start.16 = (bf16[2,2,256,128]{3,2,1,0:T(8,128)(2,1)S(1)}, bf16[2,2,256,128]{3,2,1,0:T(8,128)(2,1)S(1)}, u32[]{:S(2)}, u32[]{:S(2)}) collective-permute-start(bf16[2,2,256,128]{3,2,1,0:T(8,128)(2,1)S(1)} %get-tuple-element.61), channel_id=1, source_target_pairs={{0,14},{2,12},{4,10},{6,8},{8,6},{10,4},{12,2},{14,0},{1,15},{3,13... | collective-permute-start | bytes 786440 | tf_op jit(solution)/shard_map/ppermute | solution.py:486
  106.5 21.5 %shard_map.85 = (bf16[2,2,2,256,128]{4,3,2,1,0:T(8,128)(2,1)S(1)}, f32[16,256,128]{2,1,0:T(8,128)S(1)}, f32[16,256,128]{2,1,0:T(8,128)S(1)}) custom-call(s32[8]{0:T(128)S(1)} %broadcast_xor_fusion.globals_ref, bf16[2,2,256,128]{3,2,1,0:T(8,128)(2,1)S(1)} %collective-permute-done.10.refs_0_, bf16[2,2,256,128]{3,2,1,0:T(8,128)(2,1)S(1)} %collective-permute-done.11.refs_1_, ...), custom_call_target="tpu_custom_call" | custom-call | flops 20937965568 | bytes 8388608 | tf_op jit(solution)/shard_map/pallas_call | solution.py:453
  128.1 3.7 %collective-permute-start.12 = (bf16[2,2,256,128]{3,2,1,0:T(8,128)(2,1)S(1)}, bf16[2,2,256,128]{3,2,1,0:T(8,128)(2,1)S(1)}, u32[]{:S(2)}, u32[]{:S(2)}) collective-permute-start(bf16[2,2,256,128]{3,2,1,0:T(8,128)(2,1)S(1)} %get-tuple-element.111), channel_id=1, source_target_pairs={{0,8},{2,10},{4,12},{6,14},{8,0},{10,2},{12,4},{14,6},{1,9},{3,11}... | collective-permute-start | bytes 786440 | tf_op jit(solution)/shard_map/ppermute | solution.py:486
  131.9 23.1 %shard_map.86 = (bf16[2,2,2,256,128]{4,3,2,1,0:T(8,128)(2,1)S(1)}, f32[16,256,128]{2,1,0:T(8,128)S(1)}, f32[16,256,128]{2,1,0:T(8,128)S(1)}) custom-call(s32[8]{0:T(128)S(1)} %broadcast_xor_fusion.globals_ref, bf16[2,2,256,128]{3,2,1,0:T(8,128)(2,1)S(1)} %collective-permute-done.15.refs_0_, bf16[2,2,256,128]{3,2,1,0:T(8,128)(2,1)S(1)} %collective-permute-done.16.refs_1_, ...), custom_call_target="tpu_custom_call" | custom-call | flops 20937965568 | bytes 8388608 | tf_op jit(solution)/shard_map/pallas_call | solution.py:453
  157.3 16.7 %shard_map.87 = (bf16[2,2,2,256,128]{4,3,2,1,0:T(8,128)(2,1)S(1)}, bf16[8,2,2,256,128]{4,3,2,1,0:T(8,128)(2,1)S(1)}) custom-call(s32[8]{0:T(128)S(1)} %broadcast_xor_fusion.globals_ref, bf16[2,2,256,128]{3,2,1,0:T(8,128)(2,1)S(1)} %collective-permute-done.9.refs_0_, bf16[2,2,256,128]{3,2,1,0:T(8,128)(2,1)S(1)} %collective-permute-done.14.refs_1_, ...), custom_call_target="tpu_custom_call" | custom-call | flops 20937965568 | bytes 8388608 | tf_op jit(solution)/shard_map/pallas_call | solution.py:453
  176.3 3.2 %collective-permute-start.20 = (bf16[2,2,256,128]{3,2,1,0:T(8,128)(2,1)S(1)}, bf16[2,2,256,128]{3,2,1,0:T(8,128)(2,1)S(1)}, u32[]{:S(2)}, u32[]{:S(2)}) collective-permute-start(bf16[2,2,256,128]{3,2,1,0:T(8,128)(2,1)S(1)} %get-tuple-element.71), channel_id=1, source_target_pairs={{0,4},{2,6},{4,0},{6,2},{8,12},{10,14},{12,8},{14,10},{1,5},{3,7},... | collective-permute-start | bytes 786440 | tf_op jit(solution)/shard_map/ppermute | solution.py:486
  180.4 5.3 %collective-permute-start.24 = (bf16[2,2,256,128]{3,2,1,0:T(8,128)(2,1)S(1)}, bf16[2,2,256,128]{3,2,1,0:T(8,128)(2,1)S(1)}, u32[]{:S(2)}, u32[]{:S(2)}) collective-permute-start(bf16[2,2,256,128]{3,2,1,0:T(8,128)(2,1)S(1)} %get-tuple-element.74), channel_id=1, source_target_pairs={{0,8},{2,10},{4,12},{6,14},{8,0},{10,2},{12,4},{14,6},{1,9},{3,11}... | collective-permute-start | bytes 786440 | tf_op jit(solution)/shard_map/ppermute | solution.py:486
  187.3 3.8 %collective-permute-done.20 = bf16[2,2,256,128]{3,2,1,0:T(8,128)(2,1)S(1)} collective-permute-done((bf16[2,2,256,128]{3,2,1,0:T(8,128)(2,1)S(1)}, bf16[2,2,256,128]{3,2,1,0:T(8,128)(2,1)S(1)}, u32[]{:S(2)}, u32[]{:S(2)}) %collective-permute-start.20) | collective-permute-done | bytes 262176 | tf_op jit(solution)/shard_map/ppermute | solution.py:486
  193.5 4.3 %collective-permute-done.23 = bf16[2,2,256,128]{3,2,1,0:T(8,128)(2,1)S(1)} collective-permute-done((bf16[2,2,256,128]{3,2,1,0:T(8,128)(2,1)S(1)}, bf16[2,2,256,128]{3,2,1,0:T(8,128)(2,1)S(1)}, u32[]{:S(2)}, u32[]{:S(2)}) %collective-permute-start.23) | collective-permute-done | bytes 262176 | tf_op jit(solution)/shard_map/ppermute | solution.py:486
  197.8 3.9 %collective-permute-start.22 = (bf16[2,2,256,128]{3,2,1,0:T(8,128)(2,1)S(1)}, bf16[2,2,256,128]{3,2,1,0:T(8,128)(2,1)S(1)}, u32[]{:S(2)}, u32[]{:S(2)}) collective-permute-start(bf16[2,2,256,128]{3,2,1,0:T(8,128)(2,1)S(1)} %get-tuple-element.106), channel_id=1, source_target_pairs={{0,6},{2,4},{4,2},{6,0},{8,14},{10,12},{12,10},{14,8},{1,7},{3,5},... | collective-permute-start | bytes 786440 | tf_op jit(solution)/shard_map/ppermute | solution.py:486
  201.7 11.7 %collective-permute-done.24 = bf16[2,2,256,128]{3,2,1,0:T(8,128)(2,1)S(1)} collective-permute-done((bf16[2,2,256,128]{3,2,1,0:T(8,128)(2,1)S(1)}, bf16[2,2,256,128]{3,2,1,0:T(8,128)(2,1)S(1)}, u32[]{:S(2)}, u32[]{:S(2)}) %collective-permute-start.24) | collective-permute-done | bytes 262176 | tf_op jit(solution)/shard_map/ppermute | solution.py:486
  213.4 5.1 %collective-permute-done.25 = bf16[2,2,256,128]{3,2,1,0:T(8,128)(2,1)S(1)} collective-permute-done((bf16[2,2,256,128]{3,2,1,0:T(8,128)(2,1)S(1)}, bf16[2,2,256,128]{3,2,1,0:T(8,128)(2,1)S(1)}, u32[]{:S(2)}, u32[]{:S(2)}) %collective-permute-start.25) | collective-permute-done | bytes 262176 | tf_op jit(solution)/shard_map/ppermute | solution.py:486
  218.6 3.8 %collective-permute-done.26 = bf16[2,2,256,128]{3,2,1,0:T(8,128)(2,1)S(1)} collective-permute-done((bf16[2,2,256,128]{3,2,1,0:T(8,128)(2,1)S(1)}, bf16[2,2,256,128]{3,2,1,0:T(8,128)(2,1)S(1)}, u32[]{:S(2)}, u32[]{:S(2)}) %collective-permute-start.26) | collective-permute-done | bytes 262176 | tf_op jit(solution)/shard_map/ppermute | solution.py:486
  222.4 2.8 %collective-permute-done.27 = bf16[2,2,256,128]{3,2,1,0:T(8,128)(2,1)S(1)} collective-permute-done((bf16[2,2,256,128]{3,2,1,0:T(8,128)(2,1)S(1)}, bf16[2,2,256,128]{3,2,1,0:T(8,128)(2,1)S(1)}, u32[]{:S(2)}, u32[]{:S(2)}) %collective-permute-start.27) | collective-permute-done | bytes 262176 | tf_op jit(solution)/shard_map/ppermute | solution.py:486
  225.9 2.7 %copy_bitcast_fusion = (bf16[512,8,128]{2,1,0:T(8,128)(2,1)}, bf16[512,8,128]{2,1,0:T(8,128)(2,1)}) fusion(bf16[8,1,512,128]{3,2,1,0:T(8,128)(2,1)S(1)} %get-tuple-element.78, bf16[8,1,512,128]{3,2,1,0:T(8,128)(2,1)S(1)} %get-tuple-element.79), kind=kLoop, calls=%fused_computation | loop fusion | bytes 4194304 | tf_op jit(solution)/shard_map/transpose | solution.py:567
  (90 shorter events, 26.1 us)
Async XLA Ops:
  5.2 39.8 %collective-permute-start.5 = (bf16[2,2,256,128]{3,2,1,0:T(8,128)(2,1)}, bf16[2,2,256,128]{3,2,1,0:T(8,128)(2,1)S(1)}, u32[]{:S(2)}, u32[]{:S(2)}) collective-permute-start(bf16[2,2,256,128]{3,2,1,0:T(8,128)(2,1)} %get-tuple-element.100), channel_id=1, source_target_pairs={{0,10},{2,8},{4,14},{6,12},{8,2},{10,0},{12,6},{14,4},{1,11},{3,9}... | collective-permute-start | bytes 786440 | tf_op jit(solution)/shard_map/ppermute | solution.py:486
  7.7 43.2 %collective-permute-start.4 = (bf16[2,2,256,128]{3,2,1,0:T(8,128)(2,1)}, bf16[2,2,256,128]{3,2,1,0:T(8,128)(2,1)S(1)}, u32[]{:S(2)}, u32[]{:S(2)}) collective-permute-start(bf16[2,2,256,128]{3,2,1,0:T(8,128)(2,1)} %get-tuple-element.101), channel_id=1, source_target_pairs={{0,8},{2,10},{4,12},{6,14},{8,0},{10,2},{12,4},{14,6},{1,9},{3,11}... | collective-permute-start | bytes 786440 | tf_op jit(solution)/shard_map/ppermute | solution.py:486
  17.3 14.8 %collective-permute-start.1 = (bf16[2,2,256,128]{3,2,1,0:T(8,128)(2,1)S(1)}, bf16[2,2,256,128]{3,2,1,0:T(8,128)(2,1)S(1)}, u32[]{:S(2)}, u32[]{:S(2)}) collective-permute-start(bf16[2,2,256,128]{3,2,1,0:T(8,128)(2,1)S(1)} %get-tuple-element.42), channel_id=1, source_target_pairs={{0,4},{2,6},{4,0},{6,2},{8,12},{10,14},{12,8},{14,10},{1,5},{3,7},... | collective-permute-start | bytes 786440 | tf_op jit(solution)/shard_map/ppermute | solution.py:486
  41.3 31.9 %collective-permute-start.7 = (bf16[2,2,256,128]{3,2,1,0:T(8,128)(2,1)}, bf16[2,2,256,128]{3,2,1,0:T(8,128)(2,1)S(1)}, u32[]{:S(2)}, u32[]{:S(2)}) collective-permute-start(bf16[2,2,256,128]{3,2,1,0:T(8,128)(2,1)} %get-tuple-element.98), channel_id=1, source_target_pairs={{0,14},{2,12},{4,10},{6,8},{8,6},{10,4},{12,2},{14,0},{1,15},{3,13... | collective-permute-start | bytes 786440 | tf_op jit(solution)/shard_map/ppermute | solution.py:486
  44.9 33.5 %collective-permute-start.6 = (bf16[2,2,256,128]{3,2,1,0:T(8,128)(2,1)}, bf16[2,2,256,128]{3,2,1,0:T(8,128)(2,1)S(1)}, u32[]{:S(2)}, u32[]{:S(2)}) collective-permute-start(bf16[2,2,256,128]{3,2,1,0:T(8,128)(2,1)} %get-tuple-element.99), channel_id=1, source_target_pairs={{0,12},{2,14},{4,8},{6,10},{8,4},{10,6},{12,0},{14,2},{1,13},{3,15... | collective-permute-start | bytes 786440 | tf_op jit(solution)/shard_map/ppermute | solution.py:486
  44.9 60.8 %collective-permute-start.11 = (bf16[2,2,256,128]{3,2,1,0:T(8,128)(2,1)}, bf16[2,2,256,128]{3,2,1,0:T(8,128)(2,1)S(1)}, u32[]{:S(2)}, u32[]{:S(2)}) collective-permute-start(bf16[2,2,256,128]{3,2,1,0:T(8,128)(2,1)} %get-tuple-element.48), channel_id=1, source_target_pairs={{0,10},{2,8},{4,14},{6,12},{8,2},{10,0},{12,6},{14,4},{1,11},{3,9}... | collective-permute-start | bytes 786440 | tf_op jit(solution)/shard_map/ppermute | solution.py:486
  50.9 55.6 %collective-permute-start.10 = (bf16[2,2,256,128]{3,2,1,0:T(8,128)(2,1)}, bf16[2,2,256,128]{3,2,1,0:T(8,128)(2,1)S(1)}, u32[]{:S(2)}, u32[]{:S(2)}) collective-permute-start(bf16[2,2,256,128]{3,2,1,0:T(8,128)(2,1)} %get-tuple-element.47), channel_id=1, source_target_pairs={{0,8},{2,10},{4,12},{6,14},{8,0},{10,2},{12,4},{14,6},{1,9},{3,11}... | collective-permute-start | bytes 786440 | tf_op jit(solution)/shard_map/ppermute | solution.py:486
  50.9 77.2 %collective-permute-start.9 = (bf16[2,2,256,128]{3,2,1,0:T(8,128)(2,1)}, bf16[2,2,256,128]{3,2,1,0:T(8,128)(2,1)S(1)}, u32[]{:S(2)}, u32[]{:S(2)}) collective-permute-start(bf16[2,2,256,128]{3,2,1,0:T(8,128)(2,1)} %get-tuple-element.46), channel_id=1, source_target_pairs={{0,4},{2,6},{4,0},{6,2},{8,12},{10,14},{12,8},{14,10},{1,5},{3,7},... | collective-permute-start | bytes 786440 | tf_op jit(solution)/shard_map/ppermute | solution.py:486
  97.3 34.5 %collective-permute-start.16 = (bf16[2,2,256,128]{3,2,1,0:T(8,128)(2,1)S(1)}, bf16[2,2,256,128]{3,2,1,0:T(8,128)(2,1)S(1)}, u32[]{:S(2)}, u32[]{:S(2)}) collective-permute-start(bf16[2,2,256,128]{3,2,1,0:T(8,128)(2,1)S(1)} %get-tuple-element.61), channel_id=1, source_target_pairs={{0,14},{2,12},{4,10},{6,8},{8,6},{10,4},{12,2},{14,0},{1,15},{3,13... | collective-permute-start | bytes 786440 | tf_op jit(solution)/shard_map/ppermute | solution.py:486
  105.7 26.2 %collective-permute-start.15 = (bf16[2,2,256,128]{3,2,1,0:T(8,128)(2,1)S(1)}, bf16[2,2,256,128]{3,2,1,0:T(8,128)(2,1)S(1)}, u32[]{:S(2)}, u32[]{:S(2)}) collective-permute-start(bf16[2,2,256,128]{3,2,1,0:T(8,128)(2,1)S(1)} %get-tuple-element.59), channel_id=1, source_target_pairs={{0,12},{2,14},{4,8},{6,10},{8,4},{10,6},{12,0},{14,2},{1,13},{3,15... | collective-permute-start | bytes 786440 | tf_op jit(solution)/shard_map/ppermute | solution.py:486
  105.8 26.1 %collective-permute-start.8 = (bf16[2,2,256,128]{3,2,1,0:T(8,128)(2,1)S(1)}, bf16[2,2,256,128]{3,2,1,0:T(8,128)(2,1)S(1)}, u32[]{:S(2)}, u32[]{:S(2)}) collective-permute-start(bf16[2,2,256,128]{3,2,1,0:T(8,128)(2,1)S(1)} %get-tuple-element.112), channel_id=1, source_target_pairs={{0,2},{2,0},{4,6},{6,4},{8,10},{10,8},{12,14},{14,12},{1,3},{3,1},... | collective-permute-start | bytes 786440 | tf_op jit(solution)/shard_map/ppermute | solution.py:486
  128.0 27.0 %collective-permute-start.13 = (bf16[2,2,256,128]{3,2,1,0:T(8,128)(2,1)S(1)}, bf16[2,2,256,128]{3,2,1,0:T(8,128)(2,1)S(1)}, u32[]{:S(2)}, u32[]{:S(2)}) collective-permute-start(bf16[2,2,256,128]{3,2,1,0:T(8,128)(2,1)S(1)} %get-tuple-element.110), channel_id=1, source_target_pairs={{0,10},{2,8},{4,14},{6,12},{8,2},{10,0},{12,6},{14,4},{1,11},{3,9}... | collective-permute-start | bytes 786440 | tf_op jit(solution)/shard_map/ppermute | solution.py:486
  128.1 26.9 %collective-permute-start.12 = (bf16[2,2,256,128]{3,2,1,0:T(8,128)(2,1)S(1)}, bf16[2,2,256,128]{3,2,1,0:T(8,128)(2,1)S(1)}, u32[]{:S(2)}, u32[]{:S(2)}) collective-permute-start(bf16[2,2,256,128]{3,2,1,0:T(8,128)(2,1)S(1)} %get-tuple-element.111), channel_id=1, source_target_pairs={{0,8},{2,10},{4,12},{6,14},{8,0},{10,2},{12,4},{14,6},{1,9},{3,11}... | collective-permute-start | bytes 786440 | tf_op jit(solution)/shard_map/ppermute | solution.py:486
  131.9 25.4 %collective-permute-start.14 = (bf16[2,2,256,128]{3,2,1,0:T(8,128)(2,1)S(1)}, bf16[2,2,256,128]{3,2,1,0:T(8,128)(2,1)S(1)}, u32[]{:S(2)}, u32[]{:S(2)}) collective-permute-start(bf16[2,2,256,128]{3,2,1,0:T(8,128)(2,1)S(1)} %get-tuple-element.57), channel_id=1, source_target_pairs={{0,6},{2,4},{4,2},{6,0},{8,14},{10,12},{12,10},{14,8},{1,7},{3,5},... | collective-permute-start | bytes 786440 | tf_op jit(solution)/shard_map/ppermute | solution.py:486
  155.1 19.1 %collective-permute-start.18 = (bf16[2,2,256,128]{3,2,1,0:T(8,128)(2,1)S(1)}, bf16[2,2,256,128]{3,2,1,0:T(8,128)(2,1)S(1)}, u32[]{:S(2)}, u32[]{:S(2)}) collective-permute-start(bf16[2,2,256,128]{3,2,1,0:T(8,128)(2,1)S(1)} %get-tuple-element.108), channel_id=1, source_target_pairs={{0,14},{2,12},{4,10},{6,8},{8,6},{10,4},{12,2},{14,0},{1,15},{3,13... | collective-permute-start | bytes 786440 | tf_op jit(solution)/shard_map/ppermute | solution.py:486
  155.2 20.5 %collective-permute-start.17 = (bf16[2,2,256,128]{3,2,1,0:T(8,128)(2,1)S(1)}, bf16[2,2,256,128]{3,2,1,0:T(8,128)(2,1)S(1)}, u32[]{:S(2)}, u32[]{:S(2)}) collective-permute-start(bf16[2,2,256,128]{3,2,1,0:T(8,128)(2,1)S(1)} %get-tuple-element.109), channel_id=1, source_target_pairs={{0,12},{2,14},{4,8},{6,10},{8,4},{10,6},{12,0},{14,2},{1,13},{3,15... | collective-permute-start | bytes 786440 | tf_op jit(solution)/shard_map/ppermute | solution.py:486
  176.3 14.7 %collective-permute-start.20 = (bf16[2,2,256,128]{3,2,1,0:T(8,128)(2,1)S(1)}, bf16[2,2,256,128]{3,2,1,0:T(8,128)(2,1)S(1)}, u32[]{:S(2)}, u32[]{:S(2)}) collective-permute-start(bf16[2,2,256,128]{3,2,1,0:T(8,128)(2,1)S(1)} %get-tuple-element.71), channel_id=1, source_target_pairs={{0,4},{2,6},{4,0},{6,2},{8,12},{10,14},{12,8},{14,10},{1,5},{3,7},... | collective-permute-start | bytes 786440 | tf_op jit(solution)/shard_map/ppermute | solution.py:486
  179.5 18.2 %collective-permute-start.23 = (bf16[2,2,256,128]{3,2,1,0:T(8,128)(2,1)S(1)}, bf16[2,2,256,128]{3,2,1,0:T(8,128)(2,1)S(1)}, u32[]{:S(2)}, u32[]{:S(2)}) collective-permute-start(bf16[2,2,256,128]{3,2,1,0:T(8,128)(2,1)S(1)} %get-tuple-element.73), channel_id=1, source_target_pairs={{0,6},{2,4},{4,2},{6,0},{8,14},{10,12},{12,10},{14,8},{1,7},{3,5},... | collective-permute-start | bytes 786440 | tf_op jit(solution)/shard_map/ppermute | solution.py:486
  180.4 33.0 %collective-permute-start.24 = (bf16[2,2,256,128]{3,2,1,0:T(8,128)(2,1)S(1)}, bf16[2,2,256,128]{3,2,1,0:T(8,128)(2,1)S(1)}, u32[]{:S(2)}, u32[]{:S(2)}) collective-permute-start(bf16[2,2,256,128]{3,2,1,0:T(8,128)(2,1)S(1)} %get-tuple-element.74), channel_id=1, source_target_pairs={{0,8},{2,10},{4,12},{6,14},{8,0},{10,2},{12,4},{14,6},{1,9},{3,11}... | collective-permute-start | bytes 786440 | tf_op jit(solution)/shard_map/ppermute | solution.py:486
  185.8 32.8 %collective-permute-start.25 = (bf16[2,2,256,128]{3,2,1,0:T(8,128)(2,1)S(1)}, bf16[2,2,256,128]{3,2,1,0:T(8,128)(2,1)S(1)}, u32[]{:S(2)}, u32[]{:S(2)}) collective-permute-start(bf16[2,2,256,128]{3,2,1,0:T(8,128)(2,1)S(1)} %get-tuple-element.75), channel_id=1, source_target_pairs={{0,10},{2,8},{4,14},{6,12},{8,2},{10,0},{12,6},{14,4},{1,11},{3,9}... | collective-permute-start | bytes 786440 | tf_op jit(solution)/shard_map/ppermute | solution.py:486
  185.8 36.5 %collective-permute-start.26 = (bf16[2,2,256,128]{3,2,1,0:T(8,128)(2,1)S(1)}, bf16[2,2,256,128]{3,2,1,0:T(8,128)(2,1)S(1)}, u32[]{:S(2)}, u32[]{:S(2)}) collective-permute-start(bf16[2,2,256,128]{3,2,1,0:T(8,128)(2,1)S(1)} %get-tuple-element.76), channel_id=1, source_target_pairs={{0,12},{2,14},{4,8},{6,10},{8,4},{10,6},{12,0},{14,2},{1,13},{3,15... | collective-permute-start | bytes 786440 | tf_op jit(solution)/shard_map/ppermute | solution.py:486
  191.1 34.2 %collective-permute-start.27 = (bf16[2,2,256,128]{3,2,1,0:T(8,128)(2,1)S(1)}, bf16[2,2,256,128]{3,2,1,0:T(8,128)(2,1)S(1)}, u32[]{:S(2)}, u32[]{:S(2)}) collective-permute-start(bf16[2,2,256,128]{3,2,1,0:T(8,128)(2,1)S(1)} %get-tuple-element.77), channel_id=1, source_target_pairs={{0,14},{2,12},{4,10},{6,8},{8,6},{10,4},{12,2},{14,0},{1,15},{3,13... | collective-permute-start | bytes 786440 | tf_op jit(solution)/shard_map/ppermute | solution.py:486
  197.8 30.8 %collective-permute-start.22 = (bf16[2,2,256,128]{3,2,1,0:T(8,128)(2,1)S(1)}, bf16[2,2,256,128]{3,2,1,0:T(8,128)(2,1)S(1)}, u32[]{:S(2)}, u32[]{:S(2)}) collective-permute-start(bf16[2,2,256,128]{3,2,1,0:T(8,128)(2,1)S(1)} %get-tuple-element.106), channel_id=1, source_target_pairs={{0,6},{2,4},{4,2},{6,0},{8,14},{10,12},{12,10},{14,8},{1,7},{3,5},... | collective-permute-start | bytes 786440 | tf_op jit(solution)/shard_map/ppermute | solution.py:486
  213.4 15.2 %collective-permute-start.21 = (bf16[2,2,256,128]{3,2,1,0:T(8,128)(2,1)S(1)}, bf16[2,2,256,128]{3,2,1,0:T(8,128)(2,1)S(1)}, u32[]{:S(2)}, u32[]{:S(2)}) collective-permute-start(bf16[2,2,256,128]{3,2,1,0:T(8,128)(2,1)S(1)} %get-tuple-element.107), channel_id=1, source_target_pairs={{0,4},{2,6},{4,0},{6,2},{8,12},{10,14},{12,8},{14,10},{1,5},{3,7},... | collective-permute-start | bytes 786440 | tf_op jit(solution)/shard_map/ppermute | solution.py:486
  (8 other events, 100.0 us)

commit v4 on v3

--- a/solution.py
+++ b/solution.py
@@ -509,16 +509,21 @@
     query_send = pack(queries, grad_out)
     quarter = seq_count // 4
     near, far = range(1, 2 * quarter), range(2 * quarter, seq_count)
-    key_parts, query_parts = [key_send[0]], [query_send[0]]
-    for distance in near:
-        key_parts.append(swap(after(key_send[distance], key_parts[-1]), distance))
-    key_parts += [swap(key_send[distance], distance) for distance in far]
-    earlier = key_parts[2 * quarter - 1]
-    for distance in near:
-        query_parts.append(swap(after(query_send[distance], earlier), distance))
-        earlier = query_parts[-1]
-    for distance in range(2 * quarter, 3 * quarter):
-        query_parts.append(swap(after(query_send[distance], key_parts[distance]), distance))
+    key_parts, query_parts = [key_send[0]], query_send[:1] + [None] * (seq_count - 1)
+    for distance in range(1, seq_count):
+        part = key_send[distance]
+        if distance in near and distance > 1:
+            part = after(part, key_parts[1])
+        key_parts.append(swap(part, distance))
+    for distance in [*range(1, quarter), *range(2 * quarter, 3 * quarter)]:
+        earlier = key_parts[1]
+        if distance in far:
+            earlier = [key_parts[distance], key_parts[distance + quarter]]
+        query_parts[distance] = swap(after(query_send[distance], earlier), distance)
+    for distance in range(quarter, 2 * quarter):
+        query_parts[distance] = swap(
+            after(query_send[distance], query_parts[max(distance - 1, 1)]), distance
+        )
     relabelled = global_blocks ^ (me * block_count)
     state = ()
     query_back = [None] * seq_count
@@ -540,7 +545,7 @@
     fixed, state = tuple(rest[:4]), tuple(rest)
     give_back(0, out)
     for distance in range(3 * quarter, seq_count):
-        query_parts.append(swap(after(query_send[distance], out), distance))
+        query_parts[distance] = swap(after(query_send[distance], out), distance)
     out, rest = attend(2 * quarter, None)
     state = fixed + tuple(rest)
     give_back(2 * quarter, out)

time: 234 us -> 216 us (0.923)
  waiting for transfers between devices: 85.7 us -> 64.1 us
  starting transfers between devices: 53.3 us -> 58 us
    ppermute x28, waiting for transfers between devices: 85.7 us -> 64.1 us  [swap(): return lax.ppermute(array, 'seq', pairs) if distance else array]
    ppermute x28, starting transfers between devices: 53.3 us -> 58 us  [swap(): return lax.ppermute(array, 'seq', pairs) if distance else array]
  transfers between devices with their start and end apart: 28 -> 28, of which waited for: 12 -> 11; matrix products, arithmetic and copies ran while one was open for 2% -> 3% of each run, Pallas kernels for 35% -> 37%
where the time goes in v4:
time: 216 us; the launch traced here: 215 us
  Pallas kernels  80.3 us (37%)
  waiting for transfers between devices  64.1 us (30%)
  starting transfers between devices  58 us (27%)
  local copies, waits for them, and re-layouts  11.7 us (5%)
    pallas_call x4, Pallas kernels, head_attention(): pl.pallas_call(functools.partial(head_kernel, level_count, inner_bits, 1....  80.3 us
    ppermute x28, waiting for transfers between devices, swap(): return lax.ppermute(array, 'seq', pairs) if distance else array  64.1 us
    ppermute x28, starting transfers between devices, swap(): return lax.ppermute(array, 'seq', pairs) if distance else array  58 us
    transpose x2, local copies, waits for them, and re-layouts, unpack(): return (ordered[:, 0].transpose(1, 0, 2), ordered[:, 1].transpose(1, 0, 2))  5.33 us
  transfers between devices with their start and end apart: 28, of which 11 were waited for; matrix products, arithmetic and copies ran while one was open for 3% of the time, Pallas kernels for 37%

profile of v4, /device:TPU:8, one launch (start us, length us, event | category | flops | bytes accessed | tf_op | source)
XLA Modules:
  0.0 215.3 jit_solution(3688614591331145729)
XLA Ops:
  6.6 4.4 %collective-permute-start.5 = (bf16[2,2,256,128]{3,2,1,0:T(8,128)(2,1)S(1)}, bf16[2,2,256,128]{3,2,1,0:T(8,128)(2,1)S(1)}, u32[]{:S(2)}, u32[]{:S(2)}) collective-permute-start(bf16[2,2,256,128]{3,2,1,0:T(8,128)(2,1)S(1)} %get-tuple-element.98), channel_id=1, source_target_pairs={{0,10},{2,8},{4,14},{6,12},{8,2},{10,0},{12,6},{14,4},{1,11},{3,9}... | collective-permute-start | bytes 786440 | tf_op jit(solution)/shard_map/ppermute | solution.py:486
  14.1 4.1 %collective-permute-done.refs_3_ = bf16[2,2,256,128]{3,2,1,0:T(8,128)(2,1)S(1)} collective-permute-done((bf16[2,2,256,128]{3,2,1,0:T(8,128)(2,1)S(1)}, bf16[2,2,256,128]{3,2,1,0:T(8,128)(2,1)S(1)}, u32[]{:S(2)}, u32[]{:S(2)}) %collective-permute-start) | collective-permute-done | bytes 262176 | tf_op jit(solution)/shard_map/ppermute | solution.py:486
  19.8 16.3 %collective-permute-done.7.refs_9_ = bf16[2,2,256,128]{3,2,1,0:T(8,128)(2,1)S(1)} collective-permute-done((bf16[2,2,256,128]{3,2,1,0:T(8,128)(2,1)S(1)}, bf16[2,2,256,128]{3,2,1,0:T(8,128)(2,1)S(1)}, u32[]{:S(2)}, u32[]{:S(2)}) %collective-permute-start.7) | collective-permute-done | bytes 262176 | tf_op jit(solution)/shard_map/ppermute | solution.py:486
  36.1 10.6 %collective-permute-done.5.refs_7_ = bf16[2,2,256,128]{3,2,1,0:T(8,128)(2,1)S(1)} collective-permute-done((bf16[2,2,256,128]{3,2,1,0:T(8,128)(2,1)S(1)}, bf16[2,2,256,128]{3,2,1,0:T(8,128)(2,1)S(1)}, u32[]{:S(2)}, u32[]{:S(2)}) %collective-permute-start.5) | collective-permute-done | bytes 262176 | tf_op jit(solution)/shard_map/ppermute | solution.py:486
  46.7 3.1 %collective-permute-start.3 = (bf16[2,2,256,128]{3,2,1,0:T(8,128)(2,1)}, bf16[2,2,256,128]{3,2,1,0:T(8,128)(2,1)S(1)}, u32[]{:S(2)}, u32[]{:S(2)}) collective-permute-start(bf16[2,2,256,128]{3,2,1,0:T(8,128)(2,1)} %get-tuple-element.42), channel_id=1, source_target_pairs={{0,6},{2,4},{4,2},{6,0},{8,14},{10,12},{12,10},{14,8},{1,7},{3,5},... | collective-permute-start | bytes 786440 | tf_op jit(solution)/shard_map/ppermute | solution.py:486
  51.1 2.8 %collective-permute-done.4.refs_6_ = bf16[2,2,256,128]{3,2,1,0:T(8,128)(2,1)S(1)} collective-permute-done((bf16[2,2,256,128]{3,2,1,0:T(8,128)(2,1)}, bf16[2,2,256,128]{3,2,1,0:T(8,128)(2,1)S(1)}, u32[]{:S(2)}, u32[]{:S(2)}) %collective-permute-start.4) | collective-permute-done | bytes 262176 | tf_op jit(solution)/shard_map/ppermute | solution.py:486
  53.9 3.8 %collective-permute-start.10 = (bf16[2,2,256,128]{3,2,1,0:T(8,128)(2,1)}, bf16[2,2,256,128]{3,2,1,0:T(8,128)(2,1)S(1)}, u32[]{:S(2)}, u32[]{:S(2)}) collective-permute-start(bf16[2,2,256,128]{3,2,1,0:T(8,128)(2,1)} %get-tuple-element.45), channel_id=1, source_target_pairs={{0,8},{2,10},{4,12},{6,14},{8,0},{10,2},{12,4},{14,6},{1,9},{3,11}... | collective-permute-start | bytes 786440 | tf_op jit(solution)/shard_map/ppermute | solution.py:486
  57.7 2.8 %collective-permute-done.3.refs_5_ = bf16[2,2,256,128]{3,2,1,0:T(8,128)(2,1)S(1)} collective-permute-done((bf16[2,2,256,128]{3,2,1,0:T(8,128)(2,1)}, bf16[2,2,256,128]{3,2,1,0:T(8,128)(2,1)S(1)}, u32[]{:S(2)}, u32[]{:S(2)}) %collective-permute-start.3) | collective-permute-done | bytes 262176 | tf_op jit(solution)/shard_map/ppermute | solution.py:486
  60.5 18.9 %shard_map.84 = (bf16[2,2,2,256,128]{4,3,2,1,0:T(8,128)(2,1)S(1)}, bf16[16,256,128]{2,1,0:T(8,128)(2,1)S(1)}, bf16[16,256,128]{2,1,0:T(8,128)(2,1)S(1)}, bf16[16...) custom-call(s32[8]{0:T(128)S(1)} %broadcast_xor_fusion.globals_ref, ...), custom_call_target="tpu_custom_call" | custom-call | flops 20937965568 | bytes 8388608 | tf_op jit(solution)/shard_map/pallas_call | solution.py:453
  79.4 5.8 %collective-permute-start.16 = (bf16[2,2,256,128]{3,2,1,0:T(8,128)(2,1)S(1)}, bf16[2,2,256,128]{3,2,1,0:T(8,128)(2,1)S(1)}, u32[]{:S(2)}, u32[]{:S(2)}) collective-permute-start(bf16[2,2,256,128]{3,2,1,0:T(8,128)(2,1)S(1)} %get-tuple-element.59), channel_id=1, source_target_pairs={{0,14},{2,12},{4,10},{6,8},{8,6},{10,4},{12,2},{14,0},{1,15},{3,13... | collective-permute-start | bytes 786440 | tf_op jit(solution)/shard_map/ppermute | solution.py:486
  86.0 19.1 %shard_map.85 = (bf16[2,2,2,256,128]{4,3,2,1,0:T(8,128)(2,1)S(1)}, f32[16,256,128]{2,1,0:T(8,128)S(1)}, f32[16,256,128]{2,1,0:T(8,128)S(1)}) custom-call(s32[8]{0:T(128)S(1)} %broadcast_xor_fusion.globals_ref, bf16[2,2,256,128]{3,2,1,0:T(8,128)(2,1)S(1)} %collective-permute-done.10.refs_0_, bf16[2,2,256,128]{3,2,1,0:T(8,128)(2,1)S(1)} %collective-permute-done.11.refs_1_, ...), custom_call_target="tpu_custom_call" | custom-call | flops 20937965568 | bytes 8388608 | tf_op jit(solution)/shard_map/pallas_call | solution.py:453
  105.2 6.1 %collective-permute-start.13 = (bf16[2,2,256,128]{3,2,1,0:T(8,128)(2,1)S(1)}, bf16[2,2,256,128]{3,2,1,0:T(8,128)(2,1)S(1)}, u32[]{:S(2)}, u32[]{:S(2)}) collective-permute-start(bf16[2,2,256,128]{3,2,1,0:T(8,128)(2,1)S(1)} %get-tuple-element.108), channel_id=1, source_target_pairs={{0,10},{2,8},{4,14},{6,12},{8,2},{10,0},{12,6},{14,4},{1,11},{3,9}... | collective-permute-start | bytes 786440 | tf_op jit(solution)/shard_map/ppermute | solution.py:486
  111.2 7.6 %collective-permute-start.14 = (bf16[2,2,256,128]{3,2,1,0:T(8,128)(2,1)S(1)}, bf16[2,2,256,128]{3,2,1,0:T(8,128)(2,1)S(1)}, u32[]{:S(2)}, u32[]{:S(2)}) collective-permute-start(bf16[2,2,256,128]{3,2,1,0:T(8,128)(2,1)S(1)} %get-tuple-element.55), channel_id=1, source_target_pairs={{0,6},{2,4},{4,2},{6,0},{8,14},{10,12},{12,10},{14,8},{1,7},{3,5},... | collective-permute-start | bytes 786440 | tf_op jit(solution)/shard_map/ppermute | solution.py:486
  118.8 20.7 %shard_map.86 = (bf16[2,2,2,256,128]{4,3,2,1,0:T(8,128)(2,1)S(1)}, f32[16,256,128]{2,1,0:T(8,128)S(1)}, f32[16,256,128]{2,1,0:T(8,128)S(1)}) custom-call(s32[8]{0:T(128)S(1)} %broadcast_xor_fusion.globals_ref, bf16[2,2,256,128]{3,2,1,0:T(8,128)(2,1)S(1)} %collective-permute-done.15.refs_0_, bf16[2,2,256,128]{3,2,1,0:T(8,128)(2,1)S(1)} %collective-permute-done.16.refs_1_, ...), custom_call_target="tpu_custom_call" | custom-call | flops 20937965568 | bytes 8388608 | tf_op jit(solution)/shard_map/pallas_call | solution.py:453
  141.2 21.5 %shard_map.87 = (bf16[2,2,2,256,128]{4,3,2,1,0:T(8,128)(2,1)S(1)}, bf16[8,2,2,256,128]{4,3,2,1,0:T(8,128)(2,1)S(1)}) custom-call(s32[8]{0:T(128)S(1)} %broadcast_xor_fusion.globals_ref, bf16[2,2,256,128]{3,2,1,0:T(8,128)(2,1)S(1)} %collective-permute-done.9.refs_0_, bf16[2,2,256,128]{3,2,1,0:T(8,128)(2,1)S(1)} %collective-permute-done.14.refs_1_, ...), custom_call_target="tpu_custom_call" | custom-call | flops 20937965568 | bytes 8388608 | tf_op jit(solution)/shard_map/pallas_call | solution.py:453
  171.4 3.0 %collective-permute-done.20 = bf16[2,2,256,128]{3,2,1,0:T(8,128)(2,1)S(1)} collective-permute-done((bf16[2,2,256,128]{3,2,1,0:T(8,128)(2,1)S(1)}, bf16[2,2,256,128]{3,2,1,0:T(8,128)(2,1)S(1)}, u32[]{:S(2)}, u32[]{:S(2)}) %collective-permute-start.20) | collective-permute-done | bytes 262176 | tf_op jit(solution)/shard_map/ppermute | solution.py:486
  176.7 4.8 %collective-permute-done.23 = bf16[2,2,256,128]{3,2,1,0:T(8,128)(2,1)S(1)} collective-permute-done((bf16[2,2,256,128]{3,2,1,0:T(8,128)(2,1)S(1)}, bf16[2,2,256,128]{3,2,1,0:T(8,128)(2,1)S(1)}, u32[]{:S(2)}, u32[]{:S(2)}) %collective-permute-start.23) | collective-permute-done | bytes 262176 | tf_op jit(solution)/shard_map/ppermute | solution.py:486
  181.5 3.9 %collective-permute-start.22 = (bf16[2,2,256,128]{3,2,1,0:T(8,128)(2,1)S(1)}, bf16[2,2,256,128]{3,2,1,0:T(8,128)(2,1)S(1)}, u32[]{:S(2)}, u32[]{:S(2)}) collective-permute-start(bf16[2,2,256,128]{3,2,1,0:T(8,128)(2,1)S(1)} %get-tuple-element.104), channel_id=1, source_target_pairs={{0,6},{2,4},{4,2},{6,0},{8,14},{10,12},{12,10},{14,8},{1,7},{3,5},... | collective-permute-start | bytes 786440 | tf_op jit(solution)/shard_map/ppermute | solution.py:486
  185.4 3.5 %collective-permute-done.24 = bf16[2,2,256,128]{3,2,1,0:T(8,128)(2,1)S(1)} collective-permute-done((bf16[2,2,256,128]{3,2,1,0:T(8,128)(2,1)S(1)}, bf16[2,2,256,128]{3,2,1,0:T(8,128)(2,1)S(1)}, u32[]{:S(2)}, u32[]{:S(2)}) %collective-permute-start.24) | collective-permute-done | bytes 262176 | tf_op jit(solution)/shard_map/ppermute | solution.py:486
  188.8 3.3 %collective-permute-start.21 = (bf16[2,2,256,128]{3,2,1,0:T(8,128)(2,1)S(1)}, bf16[2,2,256,128]{3,2,1,0:T(8,128)(2,1)S(1)}, u32[]{:S(2)}, u32[]{:S(2)}) collective-permute-start(bf16[2,2,256,128]{3,2,1,0:T(8,128)(2,1)S(1)} %get-tuple-element.105), channel_id=1, source_target_pairs={{0,4},{2,6},{4,0},{6,2},{8,12},{10,14},{12,8},{14,10},{1,5},{3,7},... | collective-permute-start | bytes 786440 | tf_op jit(solution)/shard_map/ppermute | solution.py:486
  192.2 8.8 %collective-permute-done.25 = bf16[2,2,256,128]{3,2,1,0:T(8,128)(2,1)S(1)} collective-permute-done((bf16[2,2,256,128]{3,2,1,0:T(8,128)(2,1)S(1)}, bf16[2,2,256,128]{3,2,1,0:T(8,128)(2,1)S(1)}, u32[]{:S(2)}, u32[]{:S(2)}) %collective-permute-start.25) | collective-permute-done | bytes 262176 | tf_op jit(solution)/shard_map/ppermute | solution.py:486
  201.0 4.6 %collective-permute-done.26 = bf16[2,2,256,128]{3,2,1,0:T(8,128)(2,1)S(1)} collective-permute-done((bf16[2,2,256,128]{3,2,1,0:T(8,128)(2,1)S(1)}, bf16[2,2,256,128]{3,2,1,0:T(8,128)(2,1)S(1)}, u32[]{:S(2)}, u32[]{:S(2)}) %collective-permute-start.26) | collective-permute-done | bytes 262176 | tf_op jit(solution)/shard_map/ppermute | solution.py:486
  205.6 2.9 %collective-permute-done.27 = bf16[2,2,256,128]{3,2,1,0:T(8,128)(2,1)S(1)} collective-permute-done((bf16[2,2,256,128]{3,2,1,0:T(8,128)(2,1)S(1)}, bf16[2,2,256,128]{3,2,1,0:T(8,128)(2,1)S(1)}, u32[]{:S(2)}, u32[]{:S(2)}) %collective-permute-start.27) | collective-permute-done | bytes 262176 | tf_op jit(solution)/shard_map/ppermute | solution.py:486
  212.6 2.7 %copy_bitcast_fusion.2 = (bf16[512,8,128]{2,1,0:T(8,128)(2,1)}, bf16[512,8,128]{2,1,0:T(8,128)(2,1)}) fusion(bf16[8,1,512,128]{3,2,1,0:T(8,128)(2,1)S(1)} %get-tuple-element.86, bf16[8,1,512,128]{3,2,1,0:T(8,128)(2,1)S(1)} %get-tuple-element.87), kind=kLoop, calls=%fused_computation.2 | loop fusion | bytes 4194304 | tf_op jit(solution)/shard_map/transpose | solution.py:572
  (90 shorter events, 29.3 us)
Async XLA Ops:
  3.7 32.4 %collective-permute-start.7 = (bf16[2,2,256,128]{3,2,1,0:T(8,128)(2,1)S(1)}, bf16[2,2,256,128]{3,2,1,0:T(8,128)(2,1)S(1)}, u32[]{:S(2)}, u32[]{:S(2)}) collective-permute-start(bf16[2,2,256,128]{3,2,1,0:T(8,128)(2,1)S(1)} %get-tuple-element.96), channel_id=1, source_target_pairs={{0,14},{2,12},{4,10},{6,8},{8,6},{10,4},{12,2},{14,0},{1,15},{3,13... | collective-permute-start | bytes 786440 | tf_op jit(solution)/shard_map/ppermute | solution.py:486
  6.2 43.6 %collective-permute-start.6 = (bf16[2,2,256,128]{3,2,1,0:T(8,128)(2,1)}, bf16[2,2,256,128]{3,2,1,0:T(8,128)(2,1)S(1)}, u32[]{:S(2)}, u32[]{:S(2)}) collective-permute-start(bf16[2,2,256,128]{3,2,1,0:T(8,128)(2,1)} %get-tuple-element.97), channel_id=1, source_target_pairs={{0,12},{2,14},{4,8},{6,10},{8,4},{10,6},{12,0},{14,2},{1,13},{3,15... | collective-permute-start | bytes 786440 | tf_op jit(solution)/shard_map/ppermute | solution.py:486
  6.6 40.1 %collective-permute-start.5 = (bf16[2,2,256,128]{3,2,1,0:T(8,128)(2,1)S(1)}, bf16[2,2,256,128]{3,2,1,0:T(8,128)(2,1)S(1)}, u32[]{:S(2)}, u32[]{:S(2)}) collective-permute-start(bf16[2,2,256,128]{3,2,1,0:T(8,128)(2,1)S(1)} %get-tuple-element.98), channel_id=1, source_target_pairs={{0,10},{2,8},{4,14},{6,12},{8,2},{10,0},{12,6},{14,4},{1,11},{3,9}... | collective-permute-start | bytes 786440 | tf_op jit(solution)/shard_map/ppermute | solution.py:486
  11.0 42.9 %collective-permute-start.4 = (bf16[2,2,256,128]{3,2,1,0:T(8,128)(2,1)}, bf16[2,2,256,128]{3,2,1,0:T(8,128)(2,1)S(1)}, u32[]{:S(2)}, u32[]{:S(2)}) collective-permute-start(bf16[2,2,256,128]{3,2,1,0:T(8,128)(2,1)} %get-tuple-element.99), channel_id=1, source_target_pairs={{0,8},{2,10},{4,12},{6,14},{8,0},{10,2},{12,4},{14,6},{1,9},{3,11}... | collective-permute-start | bytes 786440 | tf_op jit(solution)/shard_map/ppermute | solution.py:486
  18.2 39.5 %collective-permute-start.1 = (bf16[2,2,256,128]{3,2,1,0:T(8,128)(2,1)}, bf16[2,2,256,128]{3,2,1,0:T(8,128)(2,1)S(1)}, u32[]{:S(2)}, u32[]{:S(2)}) collective-permute-start(bf16[2,2,256,128]{3,2,1,0:T(8,128)(2,1)} %get-tuple-element.40), channel_id=1, source_target_pairs={{0,2},{2,0},{4,6},{6,4},{8,10},{10,8},{12,14},{14,12},{1,3},{3,1},... | collective-permute-start | bytes 786440 | tf_op jit(solution)/shard_map/ppermute | solution.py:486
  36.1 21.6 %collective-permute-start.2 = (bf16[2,2,256,128]{3,2,1,0:T(8,128)(2,1)}, bf16[2,2,256,128]{3,2,1,0:T(8,128)(2,1)S(1)}, u32[]{:S(2)}, u32[]{:S(2)}) collective-permute-start(bf16[2,2,256,128]{3,2,1,0:T(8,128)(2,1)} %get-tuple-element.41), channel_id=1, source_target_pairs={{0,4},{2,6},{4,0},{6,2},{8,12},{10,14},{12,8},{14,10},{1,5},{3,7},... | collective-permute-start | bytes 786440 | tf_op jit(solution)/shard_map/ppermute | solution.py:486
  49.8 35.5 %collective-permute-start.11 = (bf16[2,2,256,128]{3,2,1,0:T(8,128)(2,1)}, bf16[2,2,256,128]{3,2,1,0:T(8,128)(2,1)S(1)}, u32[]{:S(2)}, u32[]{:S(2)}) collective-permute-start(bf16[2,2,256,128]{3,2,1,0:T(8,128)(2,1)} %get-tuple-element.46), channel_id=1, source_target_pairs={{0,10},{2,8},{4,14},{6,12},{8,2},{10,0},{12,6},{14,4},{1,11},{3,9}... | collective-permute-start | bytes 786440 | tf_op jit(solution)/shard_map/ppermute | solution.py:486
  53.9 32.0 %collective-permute-start.10 = (bf16[2,2,256,128]{3,2,1,0:T(8,128)(2,1)}, bf16[2,2,256,128]{3,2,1,0:T(8,128)(2,1)S(1)}, u32[]{:S(2)}, u32[]{:S(2)}) collective-permute-start(bf16[2,2,256,128]{3,2,1,0:T(8,128)(2,1)} %get-tuple-element.45), channel_id=1, source_target_pairs={{0,8},{2,10},{4,12},{6,14},{8,0},{10,2},{12,4},{14,6},{1,9},{3,11}... | collective-permute-start | bytes 786440 | tf_op jit(solution)/shard_map/ppermute | solution.py:486
  57.7 53.5 %collective-permute-start.9 = (bf16[2,2,256,128]{3,2,1,0:T(8,128)(2,1)}, bf16[2,2,256,128]{3,2,1,0:T(8,128)(2,1)S(1)}, u32[]{:S(2)}, u32[]{:S(2)}) collective-permute-start(bf16[2,2,256,128]{3,2,1,0:T(8,128)(2,1)} %get-tuple-element.44), channel_id=1, source_target_pairs={{0,4},{2,6},{4,0},{6,2},{8,12},{10,14},{12,8},{14,10},{1,5},{3,7},... | collective-permute-start | bytes 786440 | tf_op jit(solution)/shard_map/ppermute | solution.py:486
  79.4 31.8 %collective-permute-start.16 = (bf16[2,2,256,128]{3,2,1,0:T(8,128)(2,1)S(1)}, bf16[2,2,256,128]{3,2,1,0:T(8,128)(2,1)S(1)}, u32[]{:S(2)}, u32[]{:S(2)}) collective-permute-start(bf16[2,2,256,128]{3,2,1,0:T(8,128)(2,1)S(1)} %get-tuple-element.59), channel_id=1, source_target_pairs={{0,14},{2,12},{4,10},{6,8},{8,6},{10,4},{12,2},{14,0},{1,15},{3,13... | collective-permute-start | bytes 786440 | tf_op jit(solution)/shard_map/ppermute | solution.py:486
  85.2 33.6 %collective-permute-start.15 = (bf16[2,2,256,128]{3,2,1,0:T(8,128)(2,1)S(1)}, bf16[2,2,256,128]{3,2,1,0:T(8,128)(2,1)S(1)}, u32[]{:S(2)}, u32[]{:S(2)}) collective-permute-start(bf16[2,2,256,128]{3,2,1,0:T(8,128)(2,1)S(1)} %get-tuple-element.57), channel_id=1, source_target_pairs={{0,12},{2,14},{4,8},{6,10},{8,4},{10,6},{12,0},{14,2},{1,13},{3,15... | collective-permute-start | bytes 786440 | tf_op jit(solution)/shard_map/ppermute | solution.py:486
  85.3 33.6 %collective-permute-start.8 = (bf16[2,2,256,128]{3,2,1,0:T(8,128)(2,1)S(1)}, bf16[2,2,256,128]{3,2,1,0:T(8,128)(2,1)S(1)}, u32[]{:S(2)}, u32[]{:S(2)}) collective-permute-start(bf16[2,2,256,128]{3,2,1,0:T(8,128)(2,1)S(1)} %get-tuple-element.110), channel_id=1, source_target_pairs={{0,2},{2,0},{4,6},{6,4},{8,10},{10,8},{12,14},{14,12},{1,3},{3,1},... | collective-permute-start | bytes 786440 | tf_op jit(solution)/shard_map/ppermute | solution.py:486
  105.2 34.4 %collective-permute-start.13 = (bf16[2,2,256,128]{3,2,1,0:T(8,128)(2,1)S(1)}, bf16[2,2,256,128]{3,2,1,0:T(8,128)(2,1)S(1)}, u32[]{:S(2)}, u32[]{:S(2)}) collective-permute-start(bf16[2,2,256,128]{3,2,1,0:T(8,128)(2,1)S(1)} %get-tuple-element.108), channel_id=1, source_target_pairs={{0,10},{2,8},{4,14},{6,12},{8,2},{10,0},{12,6},{14,4},{1,11},{3,9}... | collective-permute-start | bytes 786440 | tf_op jit(solution)/shard_map/ppermute | solution.py:486
  111.2 28.4 %collective-permute-start.12 = (bf16[2,2,256,128]{3,2,1,0:T(8,128)(2,1)S(1)}, bf16[2,2,256,128]{3,2,1,0:T(8,128)(2,1)S(1)}, u32[]{:S(2)}, u32[]{:S(2)}) collective-permute-start(bf16[2,2,256,128]{3,2,1,0:T(8,128)(2,1)S(1)} %get-tuple-element.109), channel_id=1, source_target_pairs={{0,8},{2,10},{4,12},{6,14},{8,0},{10,2},{12,4},{14,6},{1,9},{3,11}... | collective-permute-start | bytes 786440 | tf_op jit(solution)/shard_map/ppermute | solution.py:486
  111.2 30.0 %collective-permute-start.14 = (bf16[2,2,256,128]{3,2,1,0:T(8,128)(2,1)S(1)}, bf16[2,2,256,128]{3,2,1,0:T(8,128)(2,1)S(1)}, u32[]{:S(2)}, u32[]{:S(2)}) collective-permute-start(bf16[2,2,256,128]{3,2,1,0:T(8,128)(2,1)S(1)} %get-tuple-element.55), channel_id=1, source_target_pairs={{0,6},{2,4},{4,2},{6,0},{8,14},{10,12},{12,10},{14,8},{1,7},{3,5},... | collective-permute-start | bytes 786440 | tf_op jit(solution)/shard_map/ppermute | solution.py:486
  139.7 23.3 %collective-permute-start.18 = (bf16[2,2,256,128]{3,2,1,0:T(8,128)(2,1)S(1)}, bf16[2,2,256,128]{3,2,1,0:T(8,128)(2,1)S(1)}, u32[]{:S(2)}, u32[]{:S(2)}) collective-permute-start(bf16[2,2,256,128]{3,2,1,0:T(8,128)(2,1)S(1)} %get-tuple-element.106), channel_id=1, source_target_pairs={{0,14},{2,12},{4,10},{6,8},{8,6},{10,4},{12,2},{14,0},{1,15},{3,13... | collective-permute-start | bytes 786440 | tf_op jit(solution)/shard_map/ppermute | solution.py:486
  139.7 23.2 %collective-permute-start.17 = (bf16[2,2,256,128]{3,2,1,0:T(8,128)(2,1)S(1)}, bf16[2,2,256,128]{3,2,1,0:T(8,128)(2,1)S(1)}, u32[]{:S(2)}, u32[]{:S(2)}) collective-permute-start(bf16[2,2,256,128]{3,2,1,0:T(8,128)(2,1)S(1)} %get-tuple-element.107), channel_id=1, source_target_pairs={{0,12},{2,14},{4,8},{6,10},{8,4},{10,6},{12,0},{14,2},{1,13},{3,15... | collective-permute-start | bytes 786440 | tf_op jit(solution)/shard_map/ppermute | solution.py:486
  165.0 16.4 %collective-permute-start.23 = (bf16[2,2,256,128]{3,2,1,0:T(8,128)(2,1)S(1)}, bf16[2,2,256,128]{3,2,1,0:T(8,128)(2,1)S(1)}, u32[]{:S(2)}, u32[]{:S(2)}) collective-permute-start(bf16[2,2,256,128]{3,2,1,0:T(8,128)(2,1)S(1)} %get-tuple-element.71), channel_id=1, source_target_pairs={{0,6},{2,4},{4,2},{6,0},{8,14},{10,12},{12,10},{14,8},{1,7},{3,5},... | collective-permute-start | bytes 786440 | tf_op jit(solution)/shard_map/ppermute | solution.py:486
  166.6 22.2 %collective-permute-start.24 = (bf16[2,2,256,128]{3,2,1,0:T(8,128)(2,1)S(1)}, bf16[2,2,256,128]{3,2,1,0:T(8,128)(2,1)S(1)}, u32[]{:S(2)}, u32[]{:S(2)}) collective-permute-start(bf16[2,2,256,128]{3,2,1,0:T(8,128)(2,1)S(1)} %get-tuple-element.72), channel_id=1, source_target_pairs={{0,8},{2,10},{4,12},{6,14},{8,0},{10,2},{12,4},{14,6},{1,9},{3,11}... | collective-permute-start | bytes 786440 | tf_op jit(solution)/shard_map/ppermute | solution.py:486
  169.0 31.9 %collective-permute-start.25 = (bf16[2,2,256,128]{3,2,1,0:T(8,128)(2,1)S(1)}, bf16[2,2,256,128]{3,2,1,0:T(8,128)(2,1)S(1)}, u32[]{:S(2)}, u32[]{:S(2)}) collective-permute-start(bf16[2,2,256,128]{3,2,1,0:T(8,128)(2,1)S(1)} %get-tuple-element.73), channel_id=1, source_target_pairs={{0,10},{2,8},{4,14},{6,12},{8,2},{10,0},{12,6},{14,4},{1,11},{3,9}... | collective-permute-start | bytes 786440 | tf_op jit(solution)/shard_map/ppermute | solution.py:486
  170.9 34.6 %collective-permute-start.26 = (bf16[2,2,256,128]{3,2,1,0:T(8,128)(2,1)S(1)}, bf16[2,2,256,128]{3,2,1,0:T(8,128)(2,1)S(1)}, u32[]{:S(2)}, u32[]{:S(2)}) collective-permute-start(bf16[2,2,256,128]{3,2,1,0:T(8,128)(2,1)S(1)} %get-tuple-element.74), channel_id=1, source_target_pairs={{0,12},{2,14},{4,8},{6,10},{8,4},{10,6},{12,0},{14,2},{1,13},{3,15... | collective-permute-start | bytes 786440 | tf_op jit(solution)/shard_map/ppermute | solution.py:486
  174.4 34.1 %collective-permute-start.27 = (bf16[2,2,256,128]{3,2,1,0:T(8,128)(2,1)S(1)}, bf16[2,2,256,128]{3,2,1,0:T(8,128)(2,1)S(1)}, u32[]{:S(2)}, u32[]{:S(2)}) collective-permute-start(bf16[2,2,256,128]{3,2,1,0:T(8,128)(2,1)S(1)} %get-tuple-element.75), channel_id=1, source_target_pairs={{0,14},{2,12},{4,10},{6,8},{8,6},{10,4},{12,2},{14,0},{1,15},{3,13... | collective-permute-start | bytes 786440 | tf_op jit(solution)/shard_map/ppermute | solution.py:486
  181.5 30.3 %collective-permute-start.22 = (bf16[2,2,256,128]{3,2,1,0:T(8,128)(2,1)S(1)}, bf16[2,2,256,128]{3,2,1,0:T(8,128)(2,1)S(1)}, u32[]{:S(2)}, u32[]{:S(2)}) collective-permute-start(bf16[2,2,256,128]{3,2,1,0:T(8,128)(2,1)S(1)} %get-tuple-element.104), channel_id=1, source_target_pairs={{0,6},{2,4},{4,2},{6,0},{8,14},{10,12},{12,10},{14,8},{1,7},{3,5},... | collective-permute-start | bytes 786440 | tf_op jit(solution)/shard_map/ppermute | solution.py:486
  188.8 22.9 %collective-permute-start.21 = (bf16[2,2,256,128]{3,2,1,0:T(8,128)(2,1)S(1)}, bf16[2,2,256,128]{3,2,1,0:T(8,128)(2,1)S(1)}, u32[]{:S(2)}, u32[]{:S(2)}) collective-permute-start(bf16[2,2,256,128]{3,2,1,0:T(8,128)(2,1)S(1)} %get-tuple-element.105), channel_id=1, source_target_pairs={{0,4},{2,6},{4,0},{6,2},{8,12},{10,14},{12,8},{14,10},{1,5},{3,7},... | collective-permute-start | bytes 786440 | tf_op jit(solution)/shard_map/ppermute | solution.py:486
  (8 other events, 95.7 us)
